TPU v7x, 256 devices: a whole 4x4x8 slice. The times are simulated.
256 devices in a mesh: tok: 64 (over y, z, core), grp: 4 (over x).
Axes of the slice: x: 4, y: 4, z: 8, core: 2. Of those that a mesh axis runs over, the one named last changes fastest.
Arguments:
- tokens: bfloat16 [98304, 1024], P(('tok', 'grp')), may hold values from -6 to 6
- norm_gain: float32 [1024], replicated, may hold values from 0.25 to 1.75
- input_weight: bfloat16 [1024, 3072], P('tok', 'grp')
- output_weight: bfloat16 [1024, 1024], P('tok', 'grp'), may hold values from -2 to 2
- segment_ids: int32 [98304], replicated, may hold values from 0 to 191, never falling along the last dimension, each value on 1 to 1024 neighbouring positions
- page_owner: int32 [24576, 1], P(('tok', 'grp')), may hold values from 0 to 63; in each aligned block of 96 rows (0 to 95, 96 to 191, ...) at most 3 rows name the same one
Outputs:
- attended: bfloat16 [98304, 1024], P(('tok', 'grp'))
- cache_pages: bfloat16 [49152, 8192], P(('tok', 'grp'))
Inputs may be any that keep to these rules, and one draw needn't show every extreme that they name: `segment_ids`: segment ids never fall along the pack; every id occurs on 1 to 1024 consecutive tokens, and some document has exactly 1024 tokens. `page_owner`: within the 96 pages of one device no owner is named more than 3 times, and in some device one owner is named exactly 3 times.
All inputs are finite; a program needn't handle non-finite values.
Results may differ from a plain program's by a relative error of at most 0.0089.
Values may be sent and summed in bfloat16 or wider, within the bound.
A program may use at most 128 MiB of HBM per device.

v0:
```python
import jax
import jax.numpy as jnp
from jax import lax
from jax.sharding import PartitionSpec as P

H = 16
SPAN = 1024
PAGE = 4


NEG_FILL = -1e30
ROPE_BASE = 160000.0
EPSILON = 1e-05


def shifted(value, axis, steps):
    count = lax.axis_size(axis)
    initial, last = (max(0, -steps), min(count, count - steps))
    return lax.ppermute(value, axis, [(source, source + steps) for source in range(initial, last)])


def layer_norm(tokens, norm_gain):
    values = tokens.astype(jnp.float32)
    center = jnp.mean(values, axis=-1, keepdims=True)
    spread = jnp.mean(jnp.square(values - center), axis=-1, keepdims=True)
    return ((values - center) * lax.rsqrt(spread + EPSILON) * norm_gain).astype(jnp.bfloat16)


def rotate(block_part, positions, head_count):
    row_count = block_part.shape[0]
    head_dim = block_part.shape[1] // head_count
    half_dim = head_dim // 2
    shaped = block_part.reshape(row_count, head_count, head_dim)
    inverse = 1.0 / ROPE_BASE ** (jnp.arange(half_dim, dtype=jnp.float32) * 2.0 / head_dim)
    angles = positions.astype(jnp.float32)[:, None] * inverse[None, :]
    cosine = jnp.concatenate([jnp.cos(angles), jnp.cos(angles)], axis=1)[:, None, :]
    sine_table = jnp.concatenate([jnp.sin(angles), jnp.sin(angles)], axis=1)[:, None, :]
    turned = jnp.concatenate([-shaped[..., half_dim:], shaped[..., :half_dim]], axis=-1)
    return (
        (shaped * cosine + turned * sine_table)
        .reshape(row_count, head_count * head_dim)
        .astype(jnp.bfloat16)
    )


def positions_of(segment_ids, own_ids, first_row):
    starts = jnp.searchsorted(segment_ids, own_ids, side="left")
    return first_row + jnp.arange(own_ids.shape[0], dtype=jnp.int32) - starts


def pair_scores(query_pair, key_pair, score_scale):
    return (
        jnp.einsum("tnd,snd->nts", query_pair, key_pair, preferred_element_type=jnp.float32)
        * score_scale
    )


def attend_pairs(queries, key_window, value_window, allowed, head_count):
    row_count = queries.shape[0]
    window_len = key_window.shape[0]
    head_dim = queries.shape[1] // head_count
    pair_count = head_count // 2
    score_scale = head_dim ** (-0.5)
    query_stack = jnp.transpose(queries.reshape(row_count, pair_count, 2, head_dim), (1, 0, 2, 3))
    key_stack = jnp.transpose(key_window.reshape(window_len, pair_count, 2, head_dim), (1, 0, 2, 3))
    value_stack = jnp.transpose(
        value_window.reshape(window_len, pair_count, 2, head_dim), (1, 0, 2, 3)
    )

    def one_pair(operands):
        query_pair, key_pair, value_pair = operands
        scores = jnp.where(allowed[None], pair_scores(query_pair, key_pair, score_scale), NEG_FILL)
        row_peak = jnp.max(scores, axis=-1, keepdims=True)
        exponent = jnp.exp(scores - row_peak)
        row_total = jnp.sum(exponent, axis=-1)
        weights = exponent.astype(jnp.bfloat16)
        mixed_rows = jnp.einsum(
            "nts,snd->tnd", weights, value_pair, preferred_element_type=jnp.float32
        )
        return mixed_rows / jnp.transpose(row_total)[:, :, None]

    mixed_stack = lax.map(one_pair, (query_stack, key_stack, value_stack))
    return (
        jnp.transpose(mixed_stack, (1, 0, 2, 3))
        .reshape(row_count, head_count * head_dim)
        .astype(jnp.bfloat16)
    )


def per_device(tokens, norm_gain, input_weight, output_weight, segment_ids, page_owner):
    row_count = tokens.shape[0]
    model_width = tokens.shape[1]
    device = lax.axis_index(("tok", "grp"))
    first_row = device * row_count
    normed = layer_norm(tokens, norm_gain)
    input_cols, output_cols = (
        lax.all_gather(input_weight, "grp", axis=1, tiled=True),
        lax.all_gather(output_weight, "grp", axis=1, tiled=True),
    )
    section = normed
    joined = jnp.dot(
        section,
        lax.all_gather(input_cols, "tok", axis=0, tiled=True),
        preferred_element_type=jnp.float32,
    )
    own_ids = lax.dynamic_slice_in_dim(segment_ids, first_row, row_count, 0)
    positions = positions_of(segment_ids, own_ids, first_row)
    queries = rotate(joined[:, :model_width], positions, H)
    key_rows = rotate(joined[:, model_width : 2 * model_width], positions, H)
    value_rows = joined[:, 2 * model_width :].astype(jnp.bfloat16)
    paired = jnp.stack([key_rows, value_rows])
    reach_blocks = (SPAN + row_count - 2) // row_count
    window_len = (2 * reach_blocks + 1) * row_count
    earlier = [shifted(paired, ("tok", "grp"), distance) for distance in range(reach_blocks, 0, -1)]
    later_blocks = [
        shifted(paired, ("tok", "grp"), -distance) for distance in range(1, reach_blocks + 1)
    ]
    window = jnp.concatenate(earlier + [paired] + later_blocks, axis=1)
    filler = jnp.full((reach_blocks * row_count,), -1, jnp.int32)
    padded_ids = jnp.concatenate([filler, segment_ids, filler])
    window_ids = lax.dynamic_slice_in_dim(padded_ids, first_row, window_len, 0)
    allowed = own_ids[:, None] == window_ids[None, :]
    mixed_rows = attend_pairs(queries, window[0], window[1], allowed, H)
    section = mixed_rows
    attended = jnp.dot(
        section,
        lax.all_gather(output_cols, "tok", axis=0, tiled=True),
        preferred_element_type=jnp.float32,
    ).astype(jnp.bfloat16)
    page_rows = jnp.concatenate([key_rows, value_rows], axis=1).reshape(
        row_count // PAGE, 2 * PAGE * model_width
    )
    owners = page_owner[:, 0]
    page_count = owners.shape[0]
    earlier_mask = jnp.arange(page_count)[:, None] > jnp.arange(page_count)[None, :]
    page_ranks = jnp.sum(
        ((owners[:, None] == owners[None, :]) & earlier_mask).astype(jnp.int32), axis=1
    )
    peer_count = lax.axis_size("tok")
    capacity = max(2, (2 * page_count + peer_count - 1) // peer_count)
    send_slots = jnp.zeros((peer_count * capacity, page_rows.shape[1]), jnp.bfloat16)
    send_slots = send_slots.at[owners * capacity + page_ranks].set(page_rows)
    cache_pages = lax.all_to_all(send_slots, "tok", split_axis=0, concat_axis=0, tiled=True)
    return (attended, cache_pages)


def solution(mesh):
    placed = (
        P(("tok", "grp"), None),
        P(),
        P("tok", "grp"),
        P("tok", "grp"),
        P(),
        P(("tok", "grp"), None),
    )
    return jax.shard_map(
        per_device,
        mesh=mesh,
        in_specs=placed,
        out_specs=(P(("tok", "grp"), None), P(("tok", "grp"), None)),
        check_vma=False,
    )
```

profile of v0, /device:TPU:1, one launch (start us, length us, event | category | flops | bytes accessed | tf_op | source)
XLA Modules:
  0.0 458.8 jit_solution(4806925202576879841)
XLA Ops:
  7.2 12.0 %all_gather.12 = bf16[16,3072]{1,0:T(8,128)(2,1)} all-gather(bf16[16,768]{1,0:T(8,128)(2,1)} %param.12), channel_id=1, replica_groups=mesh['tok'=64,'grp'=4] {'grp'}, dimensions={1}, use_global_device_ids=true | all-gather | bytes 122880 | tf_op jit(solution)/shard_map/all_gather | solution.py:97
  20.1 64.1 %while.36 = (s32[]{:T(128)}, u32[384]{0:T(512)S(1)}, u32[384]{0:T(512)S(1)}, s32[98304]{0:T(1024)}, s32[384]{0:T(512)S(1)}, /*index=5*/s32[]{:T(128)}, s32[]{:T(128)}, s32[]{}) while((s32[]{:T(128)}, u32[384]{0:T(512)S(1)}, u32[384]{0:T(512)S(1)}, s32[98304]{0:T(1024)}, s32[384]{0:T(512)S(1)}, /*index=5*/s32[]{:T(128)}, s32[]{:T(128)}, ...), condition=%wide.region_3.4_spmd.clone, body=%wide.region_2.3_spmd.clone.sunk | while | flops 7940 | bytes 31085 | solution.py:47
  23.8 3.7 gather_fusion
  27.6 3.7 gather_fusion
  31.4 3.7 gather_fusion
  35.2 3.7 gather_fusion
  38.9 3.7 gather_fusion
  42.7 3.7 gather_fusion
  46.5 3.7 gather_fusion
  50.2 3.7 gather_fusion
  54.0 3.7 gather_fusion
  57.8 3.7 gather_fusion
  61.5 3.7 gather_fusion
  65.3 3.7 gather_fusion
  69.1 3.7 gather_fusion
  72.8 3.8 gather_fusion
  76.7 3.7 gather_fusion
  80.5 3.7 gather_fusion
  88.8 16.0 %all-gather.3.cloned.1.call-done = bf16[1024,3072]{1,0:T(8,128)(2,1)} async-done(((bf16[16,3072]{1,0:T(8,128)(2,1)}), bf16[1024,3072]{1,0:T(8,128)(2,1)}) %all-gather.3.cloned.1.call-update) | async-done | bytes 6291472 | tf_op jit(solution)/shard_map/all_gather | solution.py:103
  104.8 5.1 %fusion.38 = f32[384,3072]{1,0:T(8,128)S(1)} fusion(bf16[1024,3072]{1,0:T(8,128)(2,1)} %all-gather.3.cloned.1.call-done, bf16[384,1024]{1,0:T(8,128)(2,1)} %param.10, f32[1024]{0:T(1024)S(1)} %copy-done.10, f32[384]{0:T(512)S(1)} %add_rsqrt_fusion, f32[384]{0:T(512)S(1)} %broadcast_multiply_fusion), kind=kOutput, calls=%fused_computation.47 | convolution fusion | flops 2417885184 | bytes 11803648 | tf_op jit(solution)/shard_map/dot_general | solution.py:101
  129.8 4.6 %add_convert_fusion = (bf16[384,1024]{1,0:T(8,128)(2,1)}, bf16[384,1024]{1,0:T(8,128)(2,1)S(1)}) fusion(f32[384,1024]{1,0:T(8,128)} %copy.26, f32[384,1024]{1,0:T(8,128)S(1)} %copy.20, f32[384,3072]{1,0:T(8,128)} %copy-done.1, f32[384,1024]{1,0:T(8,128)} %copy.22), kind=kLoop, calls=%fused_computation.44 | loop fusion | flops 2359296 | bytes 9437184 | tf_op jit(solution)/shard_map/convert_element_type | solution.py:42
  135.8 4.3 collective-permute-start
  145.6 4.3 collective-permute-start.3
  153.0 138.8 %all_gather.14 = bf16[16,1024]{1,0:T(8,128)(2,1)} all-gather(bf16[16,256]{1,0:T(8,128)(2,1)S(1)} %copy-done.9), channel_id=1, replica_groups=mesh['tok'=64,'grp'=4] {'grp'}, dimensions={1}, use_global_device_ids=true | all-gather | bytes 40960 | tf_op jit(solution)/shard_map/all_gather | solution.py:98
  299.9 4.8 %scatter_custom_fusion = bf16[192,8192]{1,0:T(8,128)(2,1)S(1)} fusion(s32[96]{0:T(128)} %fusion.46, bf16[96,8192]{1,0:T(8,128)(2,1)} %reshape.75, bf16[]{:T(256)} %constant.92.clone.1), kind=kCustom, calls=%fused_computation.42 | custom fusion | bytes 3146240 | tf_op jit(solution)/shard_map/scatter | solution.py:142
  304.7 4.4 all_to_all.8
  309.1 10.1 %all-to-all-start = ((bf16[64,3,8192]{2,1,0:T(4,128)(2,1)}), bf16[64,3,8192]{2,1,0:T(4,128)(2,1)}, u32[]{:S(2)}, u32[]{:S(2)}) async-start(bf16[64,3,8192]{2,1,0:T(4,128)(2,1)} %all_to_all.8), calls=%async_computation | async-start | bytes 8388608 | tf_op jit(solution)/shard_map/all_to_all | solution.py:143
  336.9 9.6 %fusion.47 = (bf16[1,2688,1024]{2,1,0:T(8,128)(2,1)}, bf16[1,2688,1024]{2,1,0:T(8,128)(2,1)}) fusion(bf16[2,2688,1024]{2,1,0:T(8,128)(2,1)} %constant_dynamic-update-slice_fusion), kind=kLoop, calls=%fused_computation.79 | loop fusion | bytes 22020096 | tf_op jit(solution)/shard_map/slice | solution.py:123
  346.5 8.0 %copy.28 = bf16[1,2688,1024]{1,2,0:T(8,128)(2,1)} copy(bf16[1,2688,1024]{2,1,0:T(8,128)(2,1)} %get-tuple-element.165) | data formatting | bytes 11010048 | tf_op jit(solution)/shard_map/slice | solution.py:123
  354.5 8.4 %copy.23 = bf16[1,2688,1024]{1,2,0:T(8,128)(2,1)} copy(bf16[1,2688,1024]{2,1,0:T(8,128)(2,1)} %get-tuple-element.166) | data formatting | bytes 11010048 | tf_op jit(solution)/shard_map/slice | solution.py:123
  362.9 78.1 %while.35 = (s32[]{:T(128)}, bf16[8,384,2,64]{1,3,2,0:T(8,128)(2,1)S(1)}, bf16[8,2688,2,64]{1,3,2,0:T(8,128)(2,1)}, bf16[8,384,2,64]{1,3,2,0:T(8,128)(2,1)}, bf1...) while((s32[]{:T(128)}, ...), condition=%wide.region_7.8_spmd.clone, body=%wide.region_4.7_spmd.clone.sunk | while | flops 552270336 | bytes 30602324 | solution.py:82
  444.5 7.4 %all_to_all.10 = bf16[192,8192]{1,0:T(8,128)(2,1)} reshape(bf16[64,3,8192]{2,1,0:T(4,128)(2,1)} %all-to-all-done) | data formatting | bytes 6291456 | tf_op jit(solution)/shard_map/all_to_all | solution.py:143
  (197 shorter events, 146.7 us)
Async XLA Ops:
  7.2 97.6 %all-gather.3.cloned.1.call-start = ((), (), s32[]{:S(2)}) async-start(), calls=%async_computation.1 | async-start | bytes 6389760 | tf_op jit(solution)/shard_map/all_gather | solution.py:103
  19.2 421.8 %all-gather.5.cloned.1.call-start = ((), (), s32[]{:S(2)}) async-start(), calls=%async_computation.2 | async-start | bytes 2129920 | tf_op jit(solution)/shard_map/all_gather | solution.py:127
  85.1 19.6 %copy-start.10 = (f32[1024]{0:T(1024)S(1)}, f32[1024]{0:T(1024)}, u32[]{:S(2)}) copy-start(f32[1024]{0:T(1024)} %param.11) | copy-start | bytes 12292
  109.9 3.2 copy-start.1
  113.1 21.3 %copy-start.4 = (bf16[1,384,1024]{2,1,0:T(8,128)(2,1)}, bf16[1,384,1024]{2,1,0:T(8,128)(2,1)S(1)}, u32[]{:S(2)}) copy-start(bf16[1,384,1024]{2,1,0:T(8,128)(2,1)S(1)} %slice_bitcast_fusion) | copy-start | bytes 2359300
  119.5 2.2 copy-start.8
  134.4 162.9 %copy-start.2 = (bf16[384,1024]{1,0:T(8,128)(2,1)}, bf16[384,1024]{1,0:T(8,128)(2,1)S(1)}, u32[]{:S(2)}) copy-start(bf16[384,1024]{1,0:T(8,128)(2,1)S(1)} %get-tuple-element.168) | copy-start | bytes 2359300
  134.4 18.6 %copy-start.9 = (bf16[16,256]{1,0:T(8,128)(2,1)S(1)}, bf16[16,256]{1,0:T(8,128)(2,1)}, u32[]{:S(2)}) copy-start(bf16[16,256]{1,0:T(8,128)(2,1)} %param.13) | copy-start | bytes 24580
  134.5 159.4 %copy-start = (s32[98304]{0:T(1024)S(1)}, s32[98304]{0:T(1024)}, u32[]{:S(2)}) copy-start(s32[98304]{0:T(1024)} %get-tuple-element.315) | copy-start | bytes 1179652
  134.5 159.5 %copy-start.11 = (s32[96,1]{0,1:T(1,128)S(1)}, s32[96,1]{0,1:T(1,128)}, u32[]{:S(2)}) copy-start(s32[96,1]{0,1:T(1,128)} %param.15) | copy-start | bytes 1156
  134.5 161.7 %copy-start.6 = (bf16[384,1024]{1,0:T(8,128)(2,1)S(1)}, bf16[384,1024]{1,0:T(8,128)(2,1)}, u32[]{:S(2)}) copy-start(bf16[384,1024]{1,0:T(8,128)(2,1)} %get-tuple-element.167) | copy-start | bytes 2359300
  135.8 156.1 %collective-permute-start = (bf16[2,384,1024]{2,1,0:T(8,128)(2,1)}, bf16[2,384,1024]{2,1,0:T(8,128)(2,1)}, u32[]{:S(2)}, u32[]{:S(2)}) collective-permute-start(bf16[2,384,1024]{2,1,0:T(8,128)(2,1)} %pad_maximum_fusion), channel_id=1, source_target_pairs={{0,3},{1,4},{2,5},{3,6},{4,7},{5,8},{6,9},{7,10},{8,11},{9,12},{10... | collective-permute-start | bytes 4718600 | tf_op jit(solution)/shard_map/ppermute | solution.py:19
  140.1 181.8 %collective-permute-start.1 = (bf16[2,384,1024]{2,1,0:T(8,128)(2,1)}, bf16[2,384,1024]{2,1,0:T(8,128)(2,1)}, u32[]{:S(2)}, u32[]{:S(2)}) collective-permute-start(bf16[2,384,1024]{2,1,0:T(8,128)(2,1)} %pad_maximum_fusion), channel_id=1, source_target_pairs={{0,2},{1,3},{2,4},{3,5},{4,6},{5,7},{6,8},{7,9},{8,10},{9,11},{10,... | collective-permute-start | bytes 4718600 | tf_op jit(solution)/shard_map/ppermute | solution.py:19
  143.1 181.6 %collective-permute-start.2 = (bf16[2,384,1024]{2,1,0:T(8,128)(2,1)}, bf16[2,384,1024]{2,1,0:T(8,128)(2,1)}, u32[]{:S(2)}, u32[]{:S(2)}) collective-permute-start(bf16[2,384,1024]{2,1,0:T(8,128)(2,1)} %pad_maximum_fusion), channel_id=1, source_target_pairs={{0,1},{1,2},{2,3},{3,4},{4,5},{5,6},{6,7},{7,8},{8,9},{9,10},{10,1... | collective-permute-start | bytes 4718600 | tf_op jit(solution)/shard_map/ppermute | solution.py:19
  145.6 183.2 %collective-permute-start.3 = (bf16[2,384,1024]{2,1,0:T(8,128)(2,1)}, bf16[2,384,1024]{2,1,0:T(8,128)(2,1)}, u32[]{:S(2)}, u32[]{:S(2)}) collective-permute-start(bf16[2,384,1024]{2,1,0:T(8,128)(2,1)} %pad_maximum_fusion), channel_id=1, source_target_pairs={{1,0},{2,1},{3,2},{4,3},{5,4},{6,5},{7,6},{8,7},{9,8},{10,9},{11,1... | collective-permute-start | bytes 4718600 | tf_op jit(solution)/shard_map/ppermute | solution.py:19
  149.9 181.7 %collective-permute-start.4 = (bf16[2,384,1024]{2,1,0:T(8,128)(2,1)}, bf16[2,384,1024]{2,1,0:T(8,128)(2,1)}, u32[]{:S(2)}, u32[]{:S(2)}) collective-permute-start(bf16[2,384,1024]{2,1,0:T(8,128)(2,1)} %pad_maximum_fusion), channel_id=1, source_target_pairs={{2,0},{3,1},{4,2},{5,3},{6,4},{7,5},{8,6},{9,7},{10,8},{11,9},{12,... | collective-permute-start | bytes 4718600 | tf_op jit(solution)/shard_map/ppermute | solution.py:19
  291.9 42.4 %collective-permute-start.5 = (bf16[2,384,1024]{2,1,0:T(8,128)(2,1)}, bf16[2,384,1024]{2,1,0:T(8,128)(2,1)}, u32[]{:S(2)}, u32[]{:S(2)}) collective-permute-start(bf16[2,384,1024]{2,1,0:T(8,128)(2,1)} %pad_maximum_fusion), channel_id=1, source_target_pairs={{3,0},{4,1},{5,2},{6,3},{7,4},{8,5},{9,6},{10,7},{11,8},{12,9},{13... | collective-permute-start | bytes 4718600 | tf_op jit(solution)/shard_map/ppermute | solution.py:19
  309.1 135.4 %all-to-all-start = ((bf16[64,3,8192]{2,1,0:T(4,128)(2,1)}), bf16[64,3,8192]{2,1,0:T(4,128)(2,1)}, u32[]{:S(2)}, u32[]{:S(2)}) async-start(bf16[64,3,8192]{2,1,0:T(4,128)(2,1)} %all_to_all.8), calls=%async_computation | async-start | bytes 8388608 | tf_op jit(solution)/shard_map/all_to_all | solution.py:143
  321.9 5.5 %copy-start.3 = (bf16[384,1024]{1,0:T(8,128)(2,1)S(1)}, bf16[384,1024]{1,0:T(8,128)(2,1)}, u32[]{:S(2)}) copy-start(bf16[384,1024]{1,0:T(8,128)(2,1)} %copy-done.2) | copy-start | bytes 2359300
  321.9 5.5 %copy-start.5 = (bf16[1,384,1024]{2,1,0:T(8,128)(2,1)S(1)}, bf16[1,384,1024]{2,1,0:T(8,128)(2,1)}, u32[]{:S(2)}) copy-start(bf16[1,384,1024]{2,1,0:T(8,128)(2,1)} %copy-done.4) | copy-start | bytes 2359300
  354.5 8.4 %copy-start.7 = (bf16[8,384,2,64]{1,3,2,0:T(8,128)(2,1)S(1)}, bf16[8,384,2,64]{1,3,2,0:T(8,128)(2,1)}, u32[]{:S(2)}) copy-start(bf16[8,384,2,64]{1,3,2,0:T(8,128)(2,1)} %custom-call.5) | copy-start | bytes 2359300
Sparse Core Ops, SparseCore 0:
  19.3 85.4 all-gather.2
  292.0 87.7 all-gather.4
where the time goes:
time: 461 us; the launch traced here: 459 us
  blocking collectives  151 us (33%)
  local copies, waits for them, and re-layouts  144 us (31%)
  matrix products  62.8 us (14%)
  other arithmetic  40.6 us (9%)
  starting transfers between devices  29.3 us (6%)
  waiting for transfers between devices  16.1 us (3%)
  between operations  14.3 us (3%)
    all_gather x1, blocking collectives, per_device(): lax.all_gather(output_weight, 'grp', axis=1, tiled=True)  139 us
    gather x17, local copies, waits for them, and re-layouts, positions_of(): starts = jnp.searchsorted(segment_ids, own_ids, side='left')  62.7 us
    dot_general x8, matrix products, one_pair(): jnp.einsum('nts,snd->tnd', weights, value_pair, preferred_element_type=jn...  28.6 us
    slice x3, local copies, waits for them, and re-layouts, per_device(): mixed_rows = attend_pairs(queries, window[0], window[1], allowed, H)  26 us
    dot_general x8, matrix products, pair_scores(): jnp.einsum('tnd,snd->nts', query_pair, key_pair, preferred_element_type=j...  25.6 us
    ppermute x6, starting transfers between devices, shifted(): lax.ppermute(value, axis, [(source, source + steps) for source in range(i...  19.1 us
    reduce_sum x8, other arithmetic, one_pair(): row_total = jnp.sum(exponent, axis=-1)  18.5 us
    all_gather x1, waiting for transfers between devices, per_device(): lax.all_gather(input_cols, 'tok', axis=0, tiled=True)  16 us
  transfers between devices with their start and end apart: 9, of which 1 were waited for; matrix products, arithmetic and copies ran while one was open for 45% of the time, Pallas kernels for 0%

commit v1 on v0

v1 whole, which is shorter than its diff:
```python
import functools

import jax
import jax.numpy as jnp
import ml_dtypes
import numpy as np
from jax import lax
from jax.experimental import pallas as pl
from jax.experimental.pallas import tpu as pltpu
from jax.sharding import PartitionSpec as P

D = 1024
H = 16
SPAN = 1024
PAGE = 4
CAP = 3
BLK = 384
REACH = 3
WIN = (2 * REACH + 1) * BLK
EXTRA = 256
NEG_FILL = -1e30
ROPE_BASE = 160000.0
EPSILON = 1e-5
N_TOK = 64
NY, NZ = 4, 8
ROWS = 16
TOP = 1 << 30

MESH = pl.DeviceIdType.MESH
ANY = pl.BlockSpec(memory_space=pl.ANY)
VMEM = pl.BlockSpec(memory_space=pltpu.VMEM)
SMEM = pl.BlockSpec(memory_space=pltpu.SMEM)
BF, F32 = jnp.bfloat16, jnp.float32


def rope_tables():
    freq = 1.0 / ROPE_BASE ** (np.arange(32) * 2.0 / 64)
    lanes = np.tile(freq, 4)
    out = []
    for step in (32.0, 1.0):
        angle = step * np.arange(32)[:, None] * lanes[None, :]
        rest = np.concatenate([np.cos(angle), np.sin(angle)], axis=1)
        terms = []
        for _ in range(3):
            term = rest.astype(ml_dtypes.bfloat16)
            terms.append(term)
            rest = rest - term.astype(np.float64)
        out.append(np.concatenate(terms, axis=1))
    return np.stack(out)


def mm(left, right):
    return jnp.dot(left, right, preferred_element_type=F32)


def layer_norm(values, gain):
    center = jnp.mean(values, axis=-1, keepdims=True)
    moved = values - center
    spread = jnp.mean(jnp.square(moved), axis=-1, keepdims=True)
    return moved * lax.rsqrt(spread + EPSILON) * gain


def iota(shape, axis):
    return lax.broadcasted_iota(jnp.int32, shape, axis)


def column(row):
    eye = iota((128, 128), 0) == iota((128, 128), 1)
    return jnp.sum(jnp.where(eye, jnp.broadcast_to(row, (128, 128)), 0.0), axis=1, keepdims=True)


def ids_and_places(ids_ref, chunk):
    base = pl.multiple_of(chunk * 128, 128)
    own = ids_ref[:, pl.ds(pl.multiple_of(base + SPAN, 128), 128)].astype(F32)
    col = column(own)
    total = jnp.zeros((128, 128), F32)
    for k in range(SPAN // 128 + 1):
        part = ids_ref[:, pl.ds(pl.multiple_of(base + k * 128, 128), 128)].astype(F32)
        total = total + jnp.where(jnp.broadcast_to(part, (128, 128)) < col, 1.0, 0.0)
    before = jnp.sum(total, axis=1, keepdims=True)
    place = (SPAN + iota((128, 1), 0)).astype(F32) - before
    return col, place


def turn(high, low, tab_ref):
    rows = high.shape[0]
    parts = []
    for which, value in enumerate((high, low)):
        hot = jnp.where(iota((rows, 32), 1).astype(F32) == value, 1.0, 0.0).astype(BF)
        got = mm(hot, tab_ref[which])
        parts.append(got[:, :256] + got[:, 256:512] + got[:, 512:])
    (ch, sh), (cl, sl) = [(p[:, :128], p[:, 128:]) for p in parts]
    first = lax.rem(iota((1, 128), 1), 64) < 32
    sine = sh * cl + ch * sl
    return ch * cl - sh * sl, jnp.where(first, -sine, sine)


def rotated(part, cosine, sine):
    first = lax.rem(iota((1, 128), 1), 64) < 32
    other = jnp.where(first, pltpu.roll(part, 96, 1), pltpu.roll(part, 32, 1))
    return part * cosine + other * sine


def split_place(place):
    high = jnp.floor(place * (1.0 / 32.0))
    return high, place - 32.0 * high


def slots_kernel(tok_ref, owner_row, owner_col, ids_ref, slots_ref, info_ref, wide, stage, place_all):
    pages = BLK // PAGE
    same = owner_col[...] == owner_row[...]
    earlier = iota((pages, pages), 0) < iota((pages, pages), 1)
    rank = jnp.sum(jnp.where(same & earlier, 1.0, 0.0), axis=0, keepdims=True)
    target = owner_row[...].astype(F32) * CAP + rank
    hot = jnp.where(iota((N_TOK * CAP, pages), 0).astype(F32) == target, 1.0, 0.0).astype(BF)
    for k in range(D // 128):
        wide[k] = tok_ref[:, k * 128 : k * 128 + 128].astype(F32)
    for t in range(PAGE):
        part = jnp.concatenate([wide[k, pl.ds(t, pages, stride=PAGE), :] for k in range(D // 128)], axis=1)
        placed = mm(hot, part.astype(BF))
        for k in range(D // 128):
            stage[k % 4, pl.ds(k // 4 * 4 + t, N_TOK * CAP, stride=8), :] = placed[:, k * 128 : k * 128 + 128]
    for k in range(4):
        slots_ref[:, k * 128 : k * 128 + 128] = stage[k].astype(BF)
    for k in range(BLK // 128):
        _, place = ids_and_places(ids_ref, BLK * REACH // 128 + k)
        place_all[pl.ds(k * 128, 128), :] = jnp.broadcast_to(place, (128, 128))
    lane = iota((pages, 128), 1)
    info = jnp.zeros((N_TOK, 128), F32)
    for r in range(CAP):
        packed = jnp.zeros((pages, 128), F32)
        for t in range(PAGE):
            high, low = split_place(place_all[pl.ds(t, pages, stride=PAGE), :])
            packed = jnp.where(lane == r * 8 + t * 2, high, packed)
            packed = jnp.where(lane == r * 8 + t * 2 + 1, low, packed)
        pick = jnp.where((iota((N_TOK, pages), 0) * CAP + r).astype(F32) == target, 1.0, 0.0)
        info = info + mm(pick.astype(BF), packed.astype(BF))
    info_ref[...] = info[:, None, :]


def build_slots(tokens, owner_row, owner_col, ids_row):
    return pl.pallas_call(
        slots_kernel,
        out_shape=(
            jax.ShapeDtypeStruct((N_TOK * CAP * 8, 512), BF),
            jax.ShapeDtypeStruct((N_TOK, 1, 128), F32),
        ),
        in_specs=[VMEM] * 4,
        out_specs=[VMEM] * 2,
        scratch_shapes=[
            pltpu.VMEM((D // 128, BLK, 128), F32),
            pltpu.VMEM((4, N_TOK * CAP * 8, 128), F32),
            pltpu.VMEM((BLK, 128), F32),
        ],
    )(tokens, owner_row, owner_col, ids_row)


PAIRS = 2


def main_kernel(bounds, window_ref, wqkv_hbm, wo_hbm, ids_ref, gain_ref, tab_ref, slots_hbm, info_ref,
                out_ref, cache_ref,
                tok, wqkv, wo, keys, values, heads, scores, mixed, slots, stage, sems):
    copies = [
        pltpu.make_async_copy(window_ref, tok.at[pl.ds(0, WIN)], sems.at[0]),
        pltpu.make_async_copy(wqkv_hbm, wqkv, sems.at[1]),
        pltpu.make_async_copy(slots_hbm, slots, sems.at[2]),
        pltpu.make_async_copy(wo_hbm, wo, sems.at[3]),
    ]
    for copy in copies:
        copy.start()
    gain = gain_ref[...]
    first_row = bounds[6]
    copies[0].wait()
    copies[1].wait()
    for t in range(3):
        here = pl.ds(REACH * BLK + t * 128, 128)
        normed = layer_norm(tok[here, :].astype(F32), gain).astype(BF)
        _, place = ids_and_places(ids_ref, REACH * 3 + t)
        cosine, sine = turn(*split_place(place), tab_ref)
        part = mm(normed, wqkv[:, :D])
        for pair in range(H // 2):
            turned = rotated(part[:, pair * 128 : pair * 128 + 128], cosine, sine).astype(BF) * BF(0.125)
            left = iota((128, 128), 1) < 64
            none = jnp.zeros((128, 128), BF)
            heads[t, pair, :128, :] = jnp.where(left, turned, none)
            heads[t, pair, 128:, :] = jnp.where(left, none, turned)
    low = bounds[0]
    count = (bounds[5] + 2 - low) // 2

    def project(i, _):
        chunk = low + i * 2
        start = pl.multiple_of(chunk * 128, 128)
        here = pl.ds(start, 256)
        local = start + iota((256, 1), 0)
        real = (local < WIN) & (local + first_row >= REACH * BLK) & (local + first_row < N_TOK * 4 * BLK + REACH * BLK)
        normed = jnp.where(real, layer_norm(tok[here, :].astype(F32), gain), 0.0).astype(BF)
        place = jnp.concatenate([ids_and_places(ids_ref, chunk)[1], ids_and_places(ids_ref, chunk + 1)[1]], axis=0)
        cosine, sine = turn(*split_place(place), tab_ref)
        for part in range(2):
            got = mm(normed, wqkv[:, D + part * 512 : D + part * 512 + 512])
            for k in range(4):
                lanes = pl.ds(part * 512 + k * 128, 128)
                keys[here, lanes] = rotated(got[:, k * 128 : k * 128 + 128], cosine, sine).astype(BF)
        values[here, :] = mm(normed, wqkv[:, 2 * D :]).astype(BF)
        return 0

    lax.fori_loop(0, count, project, 0)
    for t in range(3):
        id_col = column(ids_ref[:, pl.ds(SPAN + REACH * BLK + t * 128, 128)].astype(F32))
        id_col = jnp.concatenate([id_col, id_col], axis=0)
        begin = bounds[t]
        steps = (bounds[3 + t] - begin + 1) // 2

        def pairs(group, _):
            lane0 = [pl.multiple_of((group * PAIRS + j) * 128, 128) for j in range(PAIRS)]

            def score(i, peaks):
                start = pl.multiple_of((begin + i * 2) * 128, 128)
                id_row = ids_ref[:, pl.ds(pl.multiple_of(start + SPAN, 128), 256)].astype(F32)
                allowed = id_col == id_row
                new = []
                for j in range(PAIRS):
                    got = lax.dot_general(
                        heads[t, group * PAIRS + j], keys[pl.ds(start, 256), pl.ds(lane0[j], 128)],
                        (((1,), (1,)), ((), ())), preferred_element_type=F32)
                    got = jnp.where(allowed, got, NEG_FILL)
                    scores[j, i] = got
                    new.append(jnp.maximum(peaks[j], jnp.maximum(got[:, :128], got[:, 128:])))
                return tuple(new)

            peaks = lax.fori_loop(0, steps, score, (jnp.full((256, 128), NEG_FILL, F32),) * PAIRS)
            peaks = [jnp.max(p, axis=1, keepdims=True) for p in peaks]

            def mix(i, carry):
                start = pl.multiple_of((begin + i * 2) * 128, 128)
                new = []
                for j in range(PAIRS):
                    total, acc = carry[j]
                    weight = jnp.exp(scores[j, i] - peaks[j])
                    total = total + weight[:, :128] + weight[:, 128:]
                    acc = acc + mm(weight.astype(BF), values[pl.ds(start, 256), pl.ds(lane0[j], 128)])
                    new.append((total, acc))
                return tuple(new)

            zero = jnp.zeros((256, 128), F32)
            done = lax.fori_loop(0, steps, mix, ((zero, zero),) * PAIRS)
            for j in range(PAIRS):
                total, acc = done[j]
                acc = acc / jnp.sum(total, axis=1, keepdims=True)
                left = iota((128, 128), 1) < 64
                mixed[pl.ds(t * 128, 128), pl.ds(lane0[j], 128)] = jnp.where(left, acc[:128], acc[128:]).astype(BF)
            return 0

        lax.fori_loop(0, H // 2 // PAIRS, pairs, 0)
    copies[3].wait()
    out_ref[...] = mm(mixed[...], wo[...]).astype(BF)
    copies[2].wait()
    for k in range(4):
        stage[k] = slots[:, k * 128 : k * 128 + 128].astype(F32)
    count_slots = N_TOK * CAP
    info = info_ref[:, 0, :].astype(BF)
    lane = iota((count_slots, 128), 1)
    spread = []
    for r in range(CAP):
        pick = iota((count_slots, N_TOK), 0) == iota((count_slots, N_TOK), 1) * CAP + r
        spread.append(mm(jnp.where(pick, 1.0, 0.0).astype(BF), info))

    for t in range(PAGE):
        sides = [stage[k % 4, pl.ds(k // 4 * 4 + t, count_slots, stride=8), :] for k in range(8)]
        normed = layer_norm(jnp.concatenate(sides, axis=1), gain).astype(BF)
        parts = []
        for side in range(2):
            found = jnp.zeros((count_slots, 128), F32)
            for r in range(CAP):
                found = found + jnp.where(lane == r * 8 + t * 2 + side, spread[r], 0.0)
            parts.append(jnp.sum(found, axis=1, keepdims=True))
        cosine, sine = turn(*parts, tab_ref)
        got = mm(normed, wqkv[:, D : 2 * D])
        for k in range(8):
            cache_ref[:, pl.ds(t * 2048 + k * 128, 128)] = rotated(
                got[:, k * 128 : k * 128 + 128], cosine, sine).astype(BF)
        cache_ref[:, pl.ds(t * 2048 + D, D)] = mm(normed, wqkv[:, 2 * D :]).astype(BF)


def main_call(bounds, window, wqkv, wo, ids_row, gain, tables, slots, info):
    return pl.pallas_call(
        main_kernel,
        out_shape=(
            jax.ShapeDtypeStruct((BLK, D), BF),
            jax.ShapeDtypeStruct((N_TOK * CAP, 2 * PAGE * D), BF),
        ),
        in_specs=[SMEM, ANY, ANY, ANY, VMEM, VMEM, VMEM, ANY, VMEM],
        out_specs=[VMEM] * 2,
        scratch_shapes=[
            pltpu.VMEM((WIN + EXTRA, D), BF),
            pltpu.VMEM((D, 3 * D), BF),
            pltpu.VMEM((D, D), BF),
            pltpu.VMEM((WIN + EXTRA, D), BF),
            pltpu.VMEM((WIN + EXTRA, D), BF),
            pltpu.VMEM((3, H // 2, 256, 128), BF),
            pltpu.VMEM((PAIRS, 11, 256, 256), F32),
            pltpu.VMEM((BLK, D), BF),
            pltpu.VMEM((N_TOK * CAP * 8, 512), BF),
            pltpu.VMEM((4, N_TOK * CAP * 8, 128), F32),
            pltpu.SemaphoreType.DMA((4,)),
        ],
        compiler_params=pltpu.CompilerParams(vmem_limit_bytes=60 * 1024 * 1024),
    )(bounds, window, wqkv, wo, ids_row, gain, tables, slots, info)


def remote(src, dst, ssem, rsem, tok, grp):
    return pltpu.make_async_remote_copy(src_ref=src, dst_ref=dst, send_sem=ssem, recv_sem=rsem,
                                        device_id=(tok, grp), device_id_type=MESH)

def comm_kernel(tok_ref, win_ref, wout_ref, slots_ref, place_ref,
                wqkv_ref, wo_ref, window_ref, slots_out, place_out,
                xs, xr, zs, zr, ys, yr, hs, hr, bs, br, ts, tr, us, ur, ns, nr, ps, pr, loc):
    do = {"weights": True, "tokens": True, "pages": True}
    a = lax.axis_index("tok"); x = lax.axis_index("grp")
    c = lax.rem(a, 2); z = lax.rem(a // 2, NZ); y = a // (2 * NZ)
    tok_of = lambda yy, zz, cc: (yy * NZ + zz) * 2 + cc
    ring = lambda v, d, n: lax.rem(v + d + n, n)
    sib = a + 1 - 2 * c
    n_tok = NY * NZ * 2
    barrier = pltpu.get_barrier_semaphore()

    def greet(j, _):
        pl.semaphore_signal(barrier, inc=1, device_id=(lax.rem(a + j, n_tok), x), device_id_type=MESH)
        return 0
    lax.fori_loop(1, n_tok, greet, 0)
    for d in range(1, 4):
        pl.semaphore_signal(barrier, inc=1, device_id=(a, lax.rem(x + d, 4)), device_id_type=MESH)
    pl.semaphore_wait(barrier, n_tok - 1 + 3)

    weights = ((win_ref, wqkv_ref, 768), (wout_ref, wo_ref, 256))
    rows_of = lambda aa: pl.ds(pl.multiple_of(aa * 16, 16), 16)
    half_rows = lambda aa, h: pl.ds(pl.multiple_of(aa * 16 + 8 * h, 8), 8)

    xp, xm, xo = ring(x, 1, 4), ring(x, -1, 4), ring(x, 2, 4)
    widx = lambda xx, at: 3 + xx - at
    if do["weights"]:
        for w, (sh, full, cols) in enumerate(weights):
            place = full.at[rows_of(a), pl.ds(pl.multiple_of(x * cols, 128), cols)]
            pltpu.make_async_copy(sh, place, loc.at[w]).start()
            for d in range(1, 4):
                remote(sh, place, xs.at[w, d], xr.at[w, d], a, ring(x, d, 4)).start()
    if do["tokens"]:
        pltpu.make_async_copy(tok_ref, window_ref.at[3], loc.at[2]).start()
        remote(tok_ref, window_ref.at[widx(x, xp)], ts.at[0], tr.at[0], a, xp).start()
        remote(tok_ref, window_ref.at[widx(x, xm)], ts.at[1], tr.at[1], a, xm).start()
    if do["pages"]:
        mine = pl.ds(a * 3, 3)
        pltpu.make_async_copy(slots_ref.at[mine], slots_out.at[mine], loc.at[3]).start()
        pltpu.make_async_copy(place_ref.at[a], place_out.at[a], loc.at[4]).start()

        def send_pages(lo, hi):
            def one(j, _):
                peer = lax.rem(a + lax.rem(j * 27, n_tok), n_tok)
                remote(slots_ref.at[pl.ds(peer * 3, 3)], slots_out.at[mine], ps.at[0], pr.at[0], peer, x).start()
                remote(place_ref.at[peer], place_out.at[a], ps.at[1], pr.at[1], peer, x).start()
                return 0
            lax.fori_loop(lo, hi, one, 0)
    else:
        send_pages = lambda lo, hi: None
    send_pages(1, 16)

    if do["weights"]:
        def got(w, aa, sem):
            full = weights[w][1]
            remote(full.at[rows_of(aa)], full.at[rows_of(aa)], sem, sem, a, xp).wait_recv()
        def got_half(w, aa, h, sem):
            full = weights[w][1]
            remote(full.at[half_rows(aa, h)], full.at[half_rows(aa, h)], sem, sem, a, xp).wait_recv()
        def y_send(w, zz):
            full = weights[w][1]
            blk = full.at[rows_of(tok_of(y, zz, c))]
            remote(blk, blk, ys.at[w, 0, zz], yr.at[w, 0, zz], tok_of(ring(y, 1, NY), z, c), x).start()
            remote(blk, blk, ys.at[w, 1, zz], yr.at[w, 1, zz], tok_of(ring(y, -1, NY), z, c), x).start()
        def sib_send(w, yy, zz):
            full = weights[w][1]
            blk = full.at[rows_of(tok_of(yy, zz, c))]
            remote(blk, blk, bs.at[w, yy, zz], br.at[w, yy, zz], sib, x).start()
        def z_send(w, zz, dirn):
            full = weights[w][1]
            blk = full.at[rows_of(tok_of(y, zz, c))]
            remote(blk, blk, zs.at[w, dirn, zz], zr.at[w, zz], tok_of(y, ring(z, 1 - 2 * dirn, NZ), c), x).start()
        def spread(w, zz):
            y_send(w, zz)
            sib_send(w, y, zz)
        def y_relay(w, zz):
            full = weights[w][1]
            ym, yp = ring(y, -1, NY), ring(y, 1, NY)
            got(w, tok_of(ym, zz, c), yr.at[w, 0, zz])
            h = full.at[half_rows(tok_of(ym, zz, c), 0)]
            remote(h, h, hs.at[w, 0, zz], hr.at[w, 0, zz], tok_of(yp, z, c), x).start()
            sib_send(w, ym, zz)
            got(w, tok_of(yp, zz, c), yr.at[w, 1, zz])
            h = full.at[half_rows(tok_of(yp, zz, c), 1)]
            remote(h, h, hs.at[w, 1, zz], hr.at[w, 1, zz], tok_of(ym, z, c), x).start()
            sib_send(w, yp, zz)
        def y_last(w, zz):
            yo = ring(y, 2, NY)
            got_half(w, tok_of(yo, zz, c), 0, hr.at[w, 0, zz])
            got_half(w, tok_of(yo, zz, c), 1, hr.at[w, 1, zz])
            sib_send(w, yo, zz)
        W = (0, 1)
        for w in W:
            sh, full, cols = weights[w]
            place = full.at[rows_of(a), pl.ds(pl.multiple_of(x * cols, 128), cols)]
            pltpu.make_async_copy(sh, place, loc.at[w]).wait()
            for d in range(1, 4):
                src = ring(x, -d, 4)
                p = full.at[rows_of(a), pl.ds(pl.multiple_of(src * cols, 128), cols)]
                remote(sh, p, xs.at[w, d], xr.at[w, d], a, xp).wait()
        for w in W:
            z_send(w, z, 0); z_send(w, z, 1)
        for w in W:
            spread(w, z)
    send_pages(16, 24)
    if do["weights"]:
        def zstep(k, _):
            zp, zm = ring(z, -k, NZ), lax.rem(z + k, NZ)
            for w in W:
                got(w, tok_of(y, zp, c), zr.at[w, zp])
                @pl.when(k < 4)
                def _(): z_send(w, zp, 0)
            @pl.when(k < 4)
            def _():
                for w in W:
                    got(w, tok_of(y, zm, c), zr.at[w, zm])
                    @pl.when(k < 3)
                    def _(): z_send(w, zm, 1)
            for w in W:
                spread(w, zp)
            @pl.when(k < 4)
            def _():
                for w in W: spread(w, zm)
            send_pages(24 + (k - 1) * 10, 24 + k * 10)
            return 0
        lax.fori_loop(1, 5, zstep, 0)
    else:
        send_pages(24, 64)
    if do["tokens"]:
        hb = BLK // 2
        top, bot = pl.ds(0, hb), pl.ds(hb, hb)
        wfull = lambda xx, s: remote(tok_ref, window_ref.at[widx(xx, x)], tr.at[s], tr.at[s], a, xp)
        wfull(xm, 0).wait_recv()
        remote(window_ref.at[widx(xm, x), top], window_ref.at[widx(xm, xp), top], us.at[0], ur.at[0], a, xp).start()
        wfull(xp, 1).wait_recv()
        remote(window_ref.at[widx(xp, x), bot], window_ref.at[widx(xp, xm), bot], us.at[1], ur.at[1], a, xm).start()
        def cross(xx, k):
            @pl.when((xx > x) & (a < n_tok - 1))
            def _(): remote(window_ref.at[widx(xx, x)], window_ref.at[xx - x - 1], ns.at[0, k], nr.at[0, k], a + 1, x).start()
            @pl.when((xx < x) & (a > 0))
            def _(): remote(window_ref.at[widx(xx, x)], window_ref.at[xx - x + 7], ns.at[1, k], nr.at[1, k], a - 1, x).start()
        cross(xm, 0); cross(xp, 1)
    def order(i):
        return lax.rem(z + jnp.where(lax.rem(i, 2) == 1, NZ - (i + 1) // 2, i // 2), NZ)
    if do["weights"]:
        def relay(i, _):
            for w in W: y_relay(w, order(i))
            return 0
        lax.fori_loop(0, 4, relay, 0)
    if do["tokens"]:
        wh = lambda s, part: remote(window_ref.at[widx(xo, x), part], window_ref.at[widx(xo, x), part], ur.at[s], ur.at[s], a, xp)
        wh(0, top).wait_recv(); wh(1, bot).wait_recv()
        cross(xo, 2)
    if do["weights"]:
        lax.fori_loop(4, NZ, relay, 0)
        def last(i, _):
            for w in W: y_last(w, order(i))
            return 0
        lax.fori_loop(0, NZ, last, 0)
        def sibs(i, _):
            yy, zz = i // NZ, lax.rem(i, NZ)
            for w in W:
                full = weights[w][1]
                mine_blk = full.at[rows_of(tok_of(yy, zz, c))]
                blk = full.at[rows_of(tok_of(yy, zz, 1 - c))]
                remote(blk, blk, bs.at[w, yy, zz], br.at[w, yy, zz], sib, x).wait_recv()
                remote(mine_blk, mine_blk, bs.at[w, yy, zz], br.at[w, yy, zz], sib, x).wait_send()
            return 0
        lax.fori_loop(0, NY * NZ, sibs, 0)
        def drain(zz, _):
            for w in W:
                full = weights[w][1]
                blk = full.at[rows_of(a)]; h = full.at[half_rows(a, 0)]
                for d in range(2):
                    remote(blk, blk, ys.at[w, d, zz], yr.at[w, d, zz], sib, x).wait_send()
                    remote(h, h, hs.at[w, d, zz], hr.at[w, d, zz], sib, x).wait_send()
            return 0
        lax.fori_loop(0, NZ, drain, 0)
        def zdrain(k, _):
            for w in W:
                full = weights[w][1]
                blk = full.at[rows_of(a)]
                zz = ring(z, -k, NZ)
                remote(blk, blk, zs.at[w, 0, zz], zr.at[w, zz], sib, x).wait_send()
                @pl.when(k < 3)
                def _():
                    zq = lax.rem(z + k, NZ)
                    remote(blk, blk, zs.at[w, 1, zq], zr.at[w, zq], sib, x).wait_send()
            return 0
        lax.fori_loop(0, 4, zdrain, 0)
    if do["tokens"]:
        blk = window_ref.at[3]
        hv = window_ref.at[3, top]
        for d in range(2):
            remote(blk, blk, ts.at[d], tr.at[d], a, xp).wait_send()
            remote(hv, hv, us.at[d], ur.at[d], a, xp).wait_send()
        pltpu.make_async_copy(tok_ref, window_ref.at[3], loc.at[2]).wait()
        for k, xx in enumerate((xm, xp, xo)):
            up, down = (xx > x), (xx < x)
            @pl.when(up & (a < n_tok - 1))
            def _(): remote(blk, blk, ns.at[0, k], nr.at[0, k], a, xp).wait_send()
            @pl.when(down & (a > 0))
            def _(): remote(blk, blk, ns.at[1, k], nr.at[1, k], a, xp).wait_send()
            @pl.when(up & (a > 0))
            def _():
                d = window_ref.at[xx - x - 1]
                remote(d, d, ns.at[0, k], nr.at[0, k], a, xp).wait_recv()
            @pl.when(down & (a < n_tok - 1))
            def _():
                d = window_ref.at[xx - x + 7]
                remote(d, d, ns.at[1, k], nr.at[1, k], a, xp).wait_recv()
    if do["pages"]:
        pltpu.make_async_copy(slots_ref.at[mine], slots_out.at[mine], loc.at[3]).wait()
        pltpu.make_async_copy(place_ref.at[a], place_out.at[a], loc.at[4]).wait()
        rest = pl.ds(0, (n_tok - 1) * 3)
        prest = pl.ds(0, n_tok - 1)
        cp = remote(slots_ref.at[rest], slots_out.at[rest], ps.at[0], pr.at[0], a, xp); cp.wait()
        cp = remote(place_ref.at[prest], place_out.at[prest], ps.at[1], pr.at[1], a, xp); cp.wait()

def comm(tokens, w_in, w_out, slots, place):
    D = pltpu.SemaphoreType.DMA
    return pl.pallas_call(
        comm_kernel,
        out_shape=(jax.ShapeDtypeStruct((1024, 3072), BF), jax.ShapeDtypeStruct((1024, 1024), BF),
                   jax.ShapeDtypeStruct((7, tokens.shape[0], 1024), BF),
                   jax.ShapeDtypeStruct(slots.shape, BF), jax.ShapeDtypeStruct(place.shape, place.dtype)),
        in_specs=[ANY] * 5, out_specs=[ANY] * 5,
        scratch_shapes=[D((2, 4)), D((2, 4)), D((2, 2, NZ)), D((2, NZ)), D((2, 2, NZ)), D((2, 2, NZ)),
                        D((2, 2, NZ)), D((2, 2, NZ)), D((2, NY, NZ)), D((2, NY, NZ)), D((2,)), D((2,)), D((2,)), D((2,)),
                        D((2, 3)), D((2, 3)), D((2,)), D((2,)), D((5,))],
        compiler_params=pltpu.CompilerParams(collective_id=0, has_side_effects=True),
    )(tokens, w_in, w_out, slots, place)


def per_device(tokens, norm_gain, input_weight, output_weight, segment_ids, page_owner, tables):
    device = lax.axis_index("tok") * 4 + lax.axis_index("grp")
    first_row = device * BLK
    ahead = SPAN + REACH * BLK
    padded = jnp.concatenate([
        jnp.full((ahead,), -1, jnp.int32), segment_ids, jnp.full((REACH * BLK + EXTRA,), TOP, jnp.int32)])
    ids = lax.dynamic_slice_in_dim(padded, first_row, SPAN + WIN + EXTRA, 0)
    reach = ids[SPAN : SPAN + WIN]
    own = reach[REACH * BLK : (REACH + 1) * BLK].reshape(3, 128)
    begin = jnp.sum((reach[None, :] < own[:, :1]).astype(jnp.int32), axis=1) // 128
    end = (jnp.sum((reach[None, :] <= own[:, 127:]).astype(jnp.int32), axis=1) + 127) // 128
    bounds = jnp.concatenate([begin, end, first_row[None], first_row[None]])
    ids_row = ids[None, :]
    slots, info = build_slots(tokens, page_owner.reshape(1, -1), page_owner, ids_row)
    wqkv, wo, window, slots, info = comm(tokens, input_weight, output_weight, slots.reshape(N_TOK * CAP, 8, 512), info)
    return main_call(bounds, window.reshape(WIN, D), wqkv, wo, ids_row, norm_gain[None, :], tables,
                     slots.reshape(N_TOK * CAP * 8, 512), info)


def solution(mesh):
    placed = (
        P(("tok", "grp"), None),
        P(),
        P("tok", "grp"),
        P("tok", "grp"),
        P(),
        P(("tok", "grp"), None),
        P(),
    )
    tables = rope_tables()
    step = jax.shard_map(
        per_device,
        mesh=mesh,
        in_specs=placed,
        out_specs=(P(("tok", "grp"), None), P(("tok", "grp"), None)),
        check_vma=False,
    )
    return lambda *args: step(*args, jnp.asarray(tables))
```

time: 461 us -> 180 us (0.39)
  the two profiles are of different devices: /device:TPU:1 before, /device:TPU:17 now
where the time goes in v1:
time: 180 us
  Pallas kernels  175 us (97%)
  local copies, waits for them, and re-layouts  2.18 us (1%)
    pallas_call x1, Pallas kernels, comm(): pl.pallas_call(comm_kernel, out_shape=(jax.ShapeDtypeStruct((1024, 3072),...  98.6 us
    pallas_call x1, Pallas kernels, main_call(): pl.pallas_call(main_kernel, out_shape=(jax.ShapeDtypeStruct((BLK, D), BF)...  72.8 us

profile of v1, /device:TPU:17, one launch (start us, length us, event | category | flops | bytes accessed | tf_op | source)
XLA Modules:
  0.0 179.6 jit_solution(1504210303939979442)
XLA Ops:
  0.7 0.8 fusion.1
  1.5 0.2 slice_reduce_fusion.1
  1.7 0.2 convert_reduce_fusion.1
  1.9 0.6 broadcast_in_dim.21.ids_ref
  2.6 0.6 pad_add_fusion.bounds
  3.2 1.4 copy.12.owner_col
  4.5 3.5 %shard_map.86 = (bf16[1536,512]{1,0:T(8,128)(2,1)}, f32[64,1,128]{2,1,0:T(1,128)}) custom-call(bf16[384,1024]{1,0:T(8,128)(2,1)} %tok_ref.3, s32[1,96]{1,0:T(1,128)} %bitcast.12, s32[96,1]{1,0:T(8,128)} %copy.12.owner_col, s32[1,3968]{1,0:T(1,128)} %broadcast_in_dim.21.ids_ref), custom_call_target="tpu_custom_call" | custom-call | tf_op jit(solution)/shard_map/pallas_call | solution.py:142
  8.1 98.6 %shard_map.87 = (bf16[1024,3072]{1,0:T(8,128)(2,1)}, bf16[1024,1024]{1,0:T(8,128)(2,1)}, bf16[7,384,1024]{2,1,0:T(8,128)(2,1)}, bf16[192,8,512]{2,1,0:T(8,128)(2,1)}, f32[64,1,128]{2,1,0:T(1,128)}) custom-call(bf16[384,1024]{1,0:T(8,128)(2,1)} %tok_ref.3, bf16[16,768]{1,0:T(8,128)(2,1)} %win_ref.1, bf16[16,256]{1,0:T(8,128)(2,1)} %wout_ref.1, ...), custom_call_target="tpu_custom_call" | custom-call | tf_op jit(solution)/shard_map/pallas_call | solution.py:537
  106.7 72.8 %shard_map.88 = (bf16[384,1024]{1,0:T(8,128)(2,1)}, bf16[192,8192]{1,0:T(8,128)(2,1)}) custom-call(s32[8]{0:T(128)} %pad_add_fusion.bounds, bf16[2688,1024]{1,0:T(8,128)(2,1)} %bitcast.8, bf16[1024,3072]{1,0:T(8,128)(2,1)} %get-tuple-element.12.wqkv_hbm, bf16[1024,1024]{1,0:T(8,128)(2,1)} %get-tuple-element.13.wo_hbm, s32[1,3968]{1,0:T(1,128)} %broadcast_in_dim.21.ids_ref, ...), custom_call_target="tpu_custom_call" | custom-call | tf_op jit(solution)/shard_map/pallas_call | solution.py:287
  (5 shorter events, 0.0 us)

commit v2 on v1

--- a/solution.py
+++ b/solution.py
@@ -314,8 +314,8 @@
                                         device_id=(tok, grp), device_id_type=MESH)
 
 def comm_kernel(tok_ref, win_ref, wout_ref, slots_ref, place_ref,
-                wqkv_ref, wo_ref, window_ref, slots_out, place_out,
-                xs, xr, zs, zr, ys, yr, hs, hr, bs, br, ts, tr, us, ur, ns, nr, ps, pr, loc):
+                wqkv_ref, wo_ref, window_ref, slots_out, place_out, outer_ref,
+                xs, xr, zs, zr, ys, yr, hs, hr, bs, br, ts, tr, us, ur, ns, nr, os, fs, fr, ps, pr, loc):
     do = {"weights": True, "tokens": True, "pages": True}
     a = lax.axis_index("tok"); x = lax.axis_index("grp")
     c = lax.rem(a, 2); z = lax.rem(a // 2, NZ); y = a // (2 * NZ)
@@ -333,141 +333,162 @@
         pl.semaphore_signal(barrier, inc=1, device_id=(a, lax.rem(x + d, 4)), device_id_type=MESH)
     pl.semaphore_wait(barrier, n_tok - 1 + 3)
 
-    weights = ((win_ref, wqkv_ref, 768), (wout_ref, wo_ref, 256))
+    full = (wqkv_ref, wo_ref)
+    shard = (win_ref, wout_ref)
+    width = (768, 256)
+    W = (0, 1)
     rows_of = lambda aa: pl.ds(pl.multiple_of(aa * 16, 16), 16)
     half_rows = lambda aa, h: pl.ds(pl.multiple_of(aa * 16 + 8 * h, 8), 8)
-
+    block = lambda w, aa: full[w].at[rows_of(aa)]
+    half = lambda w, aa, h: full[w].at[half_rows(aa, h)]
+    piece = lambda w, aa, xx: full[w].at[rows_of(aa), pl.ds(pl.multiple_of(xx * width[w], 128), width[w])]
     xp, xm, xo = ring(x, 1, 4), ring(x, -1, 4), ring(x, 2, 4)
     widx = lambda xx, at: 3 + xx - at
+    taken = lambda ref, sem: remote(ref, ref, sem, sem, a, xp).wait_recv()
+    left = lambda ref, sem: remote(ref, ref, sem, sem, a, xp).wait_send()
+
+    def z_send(w, zz, dirn, src=None):
+        here = piece(w, tok_of(y, zz, c), x)
+        remote(here if src is None else src, here, zs.at[w, dirn, zz], zr.at[w, zz],
+               tok_of(y, ring(z, 1 - 2 * dirn, NZ), c), x).start()
+    def x_send(w, zz, src=None):
+        here = piece(w, tok_of(y, zz, c), x)
+        for d in range(1, 4):
+            remote(here if src is None else src, here, xs.at[w, d - 1, zz], xr.at[w, d - 1, zz], a, ring(x, d, 4)).start()
+    def sib_send(w, yy, zz):
+        blk = block(w, tok_of(yy, zz, c))
+        remote(blk, blk, bs.at[w, yy, zz], br.at[w, yy, zz], sib, x).start()
+    def join(w, zz):
+        for d in range(1, 4):
+            taken(piece(w, tok_of(y, zz, c), ring(x, -d, 4)), xr.at[w, d - 1, zz])
+        blk = block(w, tok_of(y, zz, c))
+        remote(blk, blk, ys.at[w, 0, zz], yr.at[w, 0, zz], tok_of(ring(y, 1, NY), z, c), x).start()
+        remote(blk, blk, ys.at[w, 1, zz], yr.at[w, 1, zz], tok_of(ring(y, -1, NY), z, c), x).start()
+        sib_send(w, y, zz)
+    def y_relay(w, zz):
+        ym, yp = ring(y, -1, NY), ring(y, 1, NY)
+        taken(block(w, tok_of(ym, zz, c)), yr.at[w, 0, zz])
+        h = half(w, tok_of(ym, zz, c), 0)
+        remote(h, h, hs.at[w, 0, zz], hr.at[w, 0, zz], tok_of(yp, z, c), x).start()
+        sib_send(w, ym, zz)
+        taken(block(w, tok_of(yp, zz, c)), yr.at[w, 1, zz])
+        h = half(w, tok_of(yp, zz, c), 1)
+        remote(h, h, hs.at[w, 1, zz], hr.at[w, 1, zz], tok_of(ym, z, c), x).start()
+        sib_send(w, yp, zz)
+    def y_last(w, zz):
+        yo = ring(y, 2, NY)
+        taken(half(w, tok_of(yo, zz, c), 0), hr.at[w, 0, zz])
+        taken(half(w, tok_of(yo, zz, c), 1), hr.at[w, 1, zz])
+        sib_send(w, yo, zz)
+    def z_step(k):
+        zp, zm = ring(z, -k, NZ), lax.rem(z + k, NZ)
+        for w in W:
+            taken(piece(w, tok_of(y, zp, c), x), zr.at[w, zp])
+            if k < 4: z_send(w, zp, 0)
+        if k < 4:
+            for w in W:
+                taken(piece(w, tok_of(y, zm, c), x), zr.at[w, zm])
+                if k < 3: z_send(w, zm, 1)
+        for w in W:
+            x_send(w, zp)
+            if k < 4: x_send(w, zm)
+    def joins(k):
+        for w in W: join(w, ring(z, -k, NZ))
+        if 0 < k < 4:
+            for w in W: join(w, lax.rem(z + k, NZ))
+
+    sgn = 1 - 2 * c
+    u = jnp.where(c == 0, x, 3 - x)
+    at_u = lambda v: jnp.where(c == 0, v, 3 - v)
+    far = a - sgn
+    linked = (far >= 0) & (far < n_tok)
+    fidx = lambda uu, at: (at_u(uu) - at_u(at)) - 1 + 8 * c
+    hb = BLK // 2
+    top, bot = pl.ds(0, hb), pl.ds(hb, hb)
+    def cross(xx, k):
+        @pl.when((xx - x) * sgn > 0)
+        def _():
+            remote(window_ref.at[widx(xx, x)], window_ref.at[xx - x - 1 + 8 * c], ns.at[k], nr.at[k], sib, x).start()
+    def outer_on():
+        @pl.when(linked & (u >= 1))
+        def _():
+            taken(outer_ref, os.at[1])
+            remote(outer_ref, window_ref.at[fidx(u, u - 1)], fs.at[0], fr.at[0], a, at_u(u - 1)).start()
+        @pl.when(linked & (u == 3))
+        def _():
+            remote(outer_ref, window_ref.at[fidx(3, 0)], fs.at[1], fr.at[1], a, at_u(0)).start()
+    def outer_relay():
+        @pl.when(linked & (u <= 2))
+        def _():
+            taken(window_ref.at[fidx(u + 1, u)], fr.at[0])
+        @pl.when(linked & (u >= 1) & (u <= 2))
+        def _():
+            remote(window_ref.at[fidx(u + 1, u)], window_ref.at[fidx(u + 1, u - 1)], fs.at[2], fr.at[2], a, at_u(u - 1)).start()
+    def ring_relay():
+        taken(window_ref.at[widx(xm, x)], tr.at[0])
+        remote(window_ref.at[widx(xm, x), top], window_ref.at[widx(xm, xp), top], us.at[0], ur.at[0], a, xp).start()
+        taken(window_ref.at[widx(xp, x)], tr.at[1])
+        remote(window_ref.at[widx(xp, x), bot], window_ref.at[widx(xp, xm), bot], us.at[1], ur.at[1], a, xm).start()
+        cross(xm, 0); cross(xp, 1)
+
+    mine = pl.ds(a * 3, 3)
+    def send_pages(lo, hi):
+        if not do["pages"]: return
+        def one(j, _):
+            peer = lax.rem(a + lax.rem(j * 27, n_tok), n_tok)
+            remote(slots_ref.at[pl.ds(peer * 3, 3)], slots_out.at[mine], ps.at[0], pr.at[0], peer, x).start()
+            remote(place_ref.at[peer], place_out.at[a], ps.at[1], pr.at[1], peer, x).start()
+            return 0
+        lax.fori_loop(lo, hi, one, 0)
+
     if do["weights"]:
-        for w, (sh, full, cols) in enumerate(weights):
-            place = full.at[rows_of(a), pl.ds(pl.multiple_of(x * cols, 128), cols)]
-            pltpu.make_async_copy(sh, place, loc.at[w]).start()
-            for d in range(1, 4):
-                remote(sh, place, xs.at[w, d], xr.at[w, d], a, ring(x, d, 4)).start()
+        for w in W:
+            pltpu.make_async_copy(shard[w], piece(w, a, x), loc.at[w]).start()
+            z_send(w, z, 0, shard[w]); z_send(w, z, 1, shard[w])
+            x_send(w, z, shard[w])
     if do["tokens"]:
         pltpu.make_async_copy(tok_ref, window_ref.at[3], loc.at[2]).start()
+        @pl.when(linked & (u <= 2))
+        def _(): remote(tok_ref, outer_ref, os.at[0], os.at[1], far, x).start()
         remote(tok_ref, window_ref.at[widx(x, xp)], ts.at[0], tr.at[0], a, xp).start()
         remote(tok_ref, window_ref.at[widx(x, xm)], ts.at[1], tr.at[1], a, xm).start()
     if do["pages"]:
-        mine = pl.ds(a * 3, 3)
         pltpu.make_async_copy(slots_ref.at[mine], slots_out.at[mine], loc.at[3]).start()
         pltpu.make_async_copy(place_ref.at[a], place_out.at[a], loc.at[4]).start()
-
-        def send_pages(lo, hi):
-            def one(j, _):
-                peer = lax.rem(a + lax.rem(j * 27, n_tok), n_tok)
-                remote(slots_ref.at[pl.ds(peer * 3, 3)], slots_out.at[mine], ps.at[0], pr.at[0], peer, x).start()
-                remote(place_ref.at[peer], place_out.at[a], ps.at[1], pr.at[1], peer, x).start()
-                return 0
-            lax.fori_loop(lo, hi, one, 0)
-    else:
-        send_pages = lambda lo, hi: None
-    send_pages(1, 16)
-
+    send_pages(1, 12)
     if do["weights"]:
-        def got(w, aa, sem):
-            full = weights[w][1]
-            remote(full.at[rows_of(aa)], full.at[rows_of(aa)], sem, sem, a, xp).wait_recv()
-        def got_half(w, aa, h, sem):
-            full = weights[w][1]
-            remote(full.at[half_rows(aa, h)], full.at[half_rows(aa, h)], sem, sem, a, xp).wait_recv()
-        def y_send(w, zz):
-            full = weights[w][1]
-            blk = full.at[rows_of(tok_of(y, zz, c))]
-            remote(blk, blk, ys.at[w, 0, zz], yr.at[w, 0, zz], tok_of(ring(y, 1, NY), z, c), x).start()
-            remote(blk, blk, ys.at[w, 1, zz], yr.at[w, 1, zz], tok_of(ring(y, -1, NY), z, c), x).start()
-        def sib_send(w, yy, zz):
-            full = weights[w][1]
-            blk = full.at[rows_of(tok_of(yy, zz, c))]
-            remote(blk, blk, bs.at[w, yy, zz], br.at[w, yy, zz], sib, x).start()
-        def z_send(w, zz, dirn):
-            full = weights[w][1]
-            blk = full.at[rows_of(tok_of(y, zz, c))]
-            remote(blk, blk, zs.at[w, dirn, zz], zr.at[w, zz], tok_of(y, ring(z, 1 - 2 * dirn, NZ), c), x).start()
-        def spread(w, zz):
-            y_send(w, zz)
-            sib_send(w, y, zz)
-        def y_relay(w, zz):
-            full = weights[w][1]
-            ym, yp = ring(y, -1, NY), ring(y, 1, NY)
-            got(w, tok_of(ym, zz, c), yr.at[w, 0, zz])
-            h = full.at[half_rows(tok_of(ym, zz, c), 0)]
-            remote(h, h, hs.at[w, 0, zz], hr.at[w, 0, zz], tok_of(yp, z, c), x).start()
-            sib_send(w, ym, zz)
-            got(w, tok_of(yp, zz, c), yr.at[w, 1, zz])
-            h = full.at[half_rows(tok_of(yp, zz, c), 1)]
-            remote(h, h, hs.at[w, 1, zz], hr.at[w, 1, zz], tok_of(ym, z, c), x).start()
-            sib_send(w, yp, zz)
-        def y_last(w, zz):
-            yo = ring(y, 2, NY)
-            got_half(w, tok_of(yo, zz, c), 0, hr.at[w, 0, zz])
-            got_half(w, tok_of(yo, zz, c), 1, hr.at[w, 1, zz])
-            sib_send(w, yo, zz)
-        W = (0, 1)
-        for w in W:
-            sh, full, cols = weights[w]
-            place = full.at[rows_of(a), pl.ds(pl.multiple_of(x * cols, 128), cols)]
-            pltpu.make_async_copy(sh, place, loc.at[w]).wait()
-            for d in range(1, 4):
-                src = ring(x, -d, 4)
-                p = full.at[rows_of(a), pl.ds(pl.multiple_of(src * cols, 128), cols)]
-                remote(sh, p, xs.at[w, d], xr.at[w, d], a, xp).wait()
-        for w in W:
-            z_send(w, z, 0); z_send(w, z, 1)
-        for w in W:
-            spread(w, z)
-    send_pages(16, 24)
+        for w in W: pltpu.make_async_copy(shard[w], piece(w, a, x), loc.at[w]).wait()
+        z_step(1); joins(0)
+    send_pages(12, 20)
     if do["weights"]:
-        def zstep(k, _):
-            zp, zm = ring(z, -k, NZ), lax.rem(z + k, NZ)
-            for w in W:
-                got(w, tok_of(y, zp, c), zr.at[w, zp])
-                @pl.when(k < 4)
-                def _(): z_send(w, zp, 0)
-            @pl.when(k < 4)
-            def _():
-                for w in W:
-                    got(w, tok_of(y, zm, c), zr.at[w, zm])
-                    @pl.when(k < 3)
-                    def _(): z_send(w, zm, 1)
-            for w in W:
-                spread(w, zp)
-            @pl.when(k < 4)
-            def _():
-                for w in W: spread(w, zm)
-            send_pages(24 + (k - 1) * 10, 24 + k * 10)
-            return 0
-        lax.fori_loop(1, 5, zstep, 0)
-    else:
-        send_pages(24, 64)
-    if do["tokens"]:
-        hb = BLK // 2
-        top, bot = pl.ds(0, hb), pl.ds(hb, hb)
-        wfull = lambda xx, s: remote(tok_ref, window_ref.at[widx(xx, x)], tr.at[s], tr.at[s], a, xp)
-        wfull(xm, 0).wait_recv()
-        remote(window_ref.at[widx(xm, x), top], window_ref.at[widx(xm, xp), top], us.at[0], ur.at[0], a, xp).start()
-        wfull(xp, 1).wait_recv()
-        remote(window_ref.at[widx(xp, x), bot], window_ref.at[widx(xp, xm), bot], us.at[1], ur.at[1], a, xm).start()
-        def cross(xx, k):
-            @pl.when((xx > x) & (a < n_tok - 1))
-            def _(): remote(window_ref.at[widx(xx, x)], window_ref.at[xx - x - 1], ns.at[0, k], nr.at[0, k], a + 1, x).start()
-            @pl.when((xx < x) & (a > 0))
-            def _(): remote(window_ref.at[widx(xx, x)], window_ref.at[xx - x + 7], ns.at[1, k], nr.at[1, k], a - 1, x).start()
-        cross(xm, 0); cross(xp, 1)
-    def order(i):
-        return lax.rem(z + jnp.where(lax.rem(i, 2) == 1, NZ - (i + 1) // 2, i // 2), NZ)
+        z_step(2); joins(1)
+    send_pages(20, 28)
+    if do["weights"]: z_step(3)
+    if do["tokens"]: outer_on()
+    send_pages(28, 36)
     if do["weights"]:
+        joins(2); z_step(4)
+    send_pages(36, 64)
+    if do["tokens"]: ring_relay()
+    if do["weights"]:
+        joins(3)
+    order = lambda i: lax.rem(z + jnp.where(lax.rem(i, 2) == 1, NZ - (i + 1) // 2, i // 2), NZ)
+    def relays(lo, hi):
         def relay(i, _):
             for w in W: y_relay(w, order(i))
             return 0
-        lax.fori_loop(0, 4, relay, 0)
+        lax.fori_loop(lo, hi, relay, 0)
+    if do["weights"]:
+        relays(0, 2)
+        joins(4)
+    if do["tokens"]: outer_relay()
+    if do["weights"]: relays(2, 5)
     if do["tokens"]:
-        wh = lambda s, part: remote(window_ref.at[widx(xo, x), part], window_ref.at[widx(xo, x), part], ur.at[s], ur.at[s], a, xp)
-        wh(0, top).wait_recv(); wh(1, bot).wait_recv()
+        taken(window_ref.at[widx(xo, x), top], ur.at[0])
+        taken(window_ref.at[widx(xo, x), bot], ur.at[1])
         cross(xo, 2)
     if do["weights"]:
-        lax.fori_loop(4, NZ, relay, 0)
+        relays(5, NZ)
         def last(i, _):
             for w in W: y_last(w, order(i))
             return 0
@@ -475,76 +496,68 @@
         def sibs(i, _):
             yy, zz = i // NZ, lax.rem(i, NZ)
             for w in W:
-                full = weights[w][1]
-                mine_blk = full.at[rows_of(tok_of(yy, zz, c))]
-                blk = full.at[rows_of(tok_of(yy, zz, 1 - c))]
-                remote(blk, blk, bs.at[w, yy, zz], br.at[w, yy, zz], sib, x).wait_recv()
-                remote(mine_blk, mine_blk, bs.at[w, yy, zz], br.at[w, yy, zz], sib, x).wait_send()
+                taken(block(w, tok_of(yy, zz, 1 - c)), br.at[w, yy, zz])
+                left(block(w, tok_of(yy, zz, c)), bs.at[w, yy, zz])
             return 0
         lax.fori_loop(0, NY * NZ, sibs, 0)
         def drain(zz, _):
             for w in W:
-                full = weights[w][1]
-                blk = full.at[rows_of(a)]; h = full.at[half_rows(a, 0)]
                 for d in range(2):
-                    remote(blk, blk, ys.at[w, d, zz], yr.at[w, d, zz], sib, x).wait_send()
-                    remote(h, h, hs.at[w, d, zz], hr.at[w, d, zz], sib, x).wait_send()
+                    left(block(w, a), ys.at[w, d, zz])
+                    left(half(w, a, 0), hs.at[w, d, zz])
+                for d in range(3):
+                    left(piece(w, a, x), xs.at[w, d, zz])
             return 0
         lax.fori_loop(0, NZ, drain, 0)
-        def zdrain(k, _):
+        for k in range(4):
             for w in W:
-                full = weights[w][1]
-                blk = full.at[rows_of(a)]
-                zz = ring(z, -k, NZ)
-                remote(blk, blk, zs.at[w, 0, zz], zr.at[w, zz], sib, x).wait_send()
-                @pl.when(k < 3)
-                def _():
-                    zq = lax.rem(z + k, NZ)
-                    remote(blk, blk, zs.at[w, 1, zq], zr.at[w, zq], sib, x).wait_send()
-            return 0
-        lax.fori_loop(0, 4, zdrain, 0)
+                left(piece(w, a, x), zs.at[w, 0, ring(z, -k, NZ)])
+                if k < 3: left(piece(w, a, x), zs.at[w, 1, lax.rem(z + k, NZ)])
     if do["tokens"]:
         blk = window_ref.at[3]
         hv = window_ref.at[3, top]
         for d in range(2):
-            remote(blk, blk, ts.at[d], tr.at[d], a, xp).wait_send()
-            remote(hv, hv, us.at[d], ur.at[d], a, xp).wait_send()
+            left(blk, ts.at[d]); left(hv, us.at[d])
         pltpu.make_async_copy(tok_ref, window_ref.at[3], loc.at[2]).wait()
         for k, xx in enumerate((xm, xp, xo)):
-            up, down = (xx > x), (xx < x)
-            @pl.when(up & (a < n_tok - 1))
-            def _(): remote(blk, blk, ns.at[0, k], nr.at[0, k], a, xp).wait_send()
-            @pl.when(down & (a > 0))
-            def _(): remote(blk, blk, ns.at[1, k], nr.at[1, k], a, xp).wait_send()
-            @pl.when(up & (a > 0))
-            def _():
-                d = window_ref.at[xx - x - 1]
-                remote(d, d, ns.at[0, k], nr.at[0, k], a, xp).wait_recv()
-            @pl.when(down & (a < n_tok - 1))
-            def _():
-                d = window_ref.at[xx - x + 7]
-                remote(d, d, ns.at[1, k], nr.at[1, k], a, xp).wait_recv()
+            @pl.when((xx - x) * sgn > 0)
+            def _(): left(blk, ns.at[k])
+            @pl.when((xx - x) * sgn < 0)
+            def _(): taken(window_ref.at[xx - x + 7 - 8 * c], nr.at[k])
+        @pl.when(linked & (u <= 2))
+        def _(): left(blk, os.at[0])
+        @pl.when(linked & (u >= 1))
+        def _(): left(blk, fs.at[0])
+        @pl.when(linked & (u == 3))
+        def _(): left(blk, fs.at[1])
+        @pl.when(linked & (u >= 1) & (u <= 2))
+        def _(): left(blk, fs.at[2])
+        @pl.when(linked & (u == 0))
+        def _(): taken(window_ref.at[fidx(3, 0)], fr.at[1])
+        @pl.when(linked & (u <= 1))
+        def _(): taken(window_ref.at[fidx(u + 2, u)], fr.at[2])
     if do["pages"]:
         pltpu.make_async_copy(slots_ref.at[mine], slots_out.at[mine], loc.at[3]).wait()
         pltpu.make_async_copy(place_ref.at[a], place_out.at[a], loc.at[4]).wait()
         rest = pl.ds(0, (n_tok - 1) * 3)
         prest = pl.ds(0, n_tok - 1)
-        cp = remote(slots_ref.at[rest], slots_out.at[rest], ps.at[0], pr.at[0], a, xp); cp.wait()
-        cp = remote(place_ref.at[prest], place_out.at[prest], ps.at[1], pr.at[1], a, xp); cp.wait()
+        remote(slots_ref.at[rest], slots_out.at[rest], ps.at[0], pr.at[0], a, xp).wait()
+        remote(place_ref.at[prest], place_out.at[prest], ps.at[1], pr.at[1], a, xp).wait()
 
 def comm(tokens, w_in, w_out, slots, place):
-    D = pltpu.SemaphoreType.DMA
+    D_ = pltpu.SemaphoreType.DMA
     return pl.pallas_call(
         comm_kernel,
         out_shape=(jax.ShapeDtypeStruct((1024, 3072), BF), jax.ShapeDtypeStruct((1024, 1024), BF),
                    jax.ShapeDtypeStruct((7, tokens.shape[0], 1024), BF),
-                   jax.ShapeDtypeStruct(slots.shape, BF), jax.ShapeDtypeStruct(place.shape, place.dtype)),
-        in_specs=[ANY] * 5, out_specs=[ANY] * 5,
-        scratch_shapes=[D((2, 4)), D((2, 4)), D((2, 2, NZ)), D((2, NZ)), D((2, 2, NZ)), D((2, 2, NZ)),
-                        D((2, 2, NZ)), D((2, 2, NZ)), D((2, NY, NZ)), D((2, NY, NZ)), D((2,)), D((2,)), D((2,)), D((2,)),
-                        D((2, 3)), D((2, 3)), D((2,)), D((2,)), D((5,))],
+                   jax.ShapeDtypeStruct(slots.shape, BF), jax.ShapeDtypeStruct(place.shape, place.dtype),
+                   jax.ShapeDtypeStruct(tokens.shape, BF)),
+        in_specs=[ANY] * 5, out_specs=[ANY] * 6,
+        scratch_shapes=[D_((2, 3, NZ)), D_((2, 3, NZ)), D_((2, 2, NZ)), D_((2, NZ)), D_((2, 2, NZ)), D_((2, 2, NZ)),
+                        D_((2, 2, NZ)), D_((2, 2, NZ)), D_((2, NY, NZ)), D_((2, NY, NZ)), D_((2,)), D_((2,)), D_((2,)), D_((2,)),
+                        D_((3,)), D_((3,)), D_((2,)), D_((3,)), D_((3,)), D_((2,)), D_((2,)), D_((5,))],
         compiler_params=pltpu.CompilerParams(collective_id=0, has_side_effects=True),
-    )(tokens, w_in, w_out, slots, place)
+    )(tokens, w_in, w_out, slots, place)[:5]
 
 
 def per_device(tokens, norm_gain, input_weight, output_weight, segment_ids, page_owner, tables):

time: 180 us -> 169 us (0.939)
  the two profiles are of different devices: /device:TPU:17 before, /device:TPU:14 now
where the time goes in v2:
time: 169 us
  Pallas kernels  164 us (97%)
  local copies, waits for them, and re-layouts  2.18 us (1%)
  other arithmetic  1.75 us (1%)
    pallas_call x1, Pallas kernels, comm(): pl.pallas_call(comm_kernel, out_shape=(jax.ShapeDtypeStruct((1024, 3072),...  81.8 us
    pallas_call x1, Pallas kernels, main_call(): pl.pallas_call(main_kernel, out_shape=(jax.ShapeDtypeStruct((BLK, D), BF)...  79 us
    pallas_call x1, Pallas kernels, build_slots(): pl.pallas_call(slots_kernel, out_shape=(jax.ShapeDtypeStruct((N_TOK * CAP...  3.54 us

profile of v2, /device:TPU:14, one launch (start us, length us, event | category | flops | bytes accessed | tf_op | source)
XLA Modules:
  0.0 169.1 jit_solution(15748180108343638536)
XLA Ops:
  0.7 0.8 fusion.1
  1.5 0.2 slice_reduce_fusion.1
  1.7 0.2 convert_reduce_fusion.1
  1.9 0.6 broadcast_in_dim.21.ids_ref
  2.6 0.7 pad_add_fusion.bounds
  3.2 1.4 copy.12.owner_col
  4.6 3.5 %shard_map.86 = (bf16[1536,512]{1,0:T(8,128)(2,1)}, f32[64,1,128]{2,1,0:T(1,128)}) custom-call(bf16[384,1024]{1,0:T(8,128)(2,1)} %tok_ref.3, s32[1,96]{1,0:T(1,128)} %bitcast.12, s32[96,1]{1,0:T(8,128)} %copy.12.owner_col, s32[1,3968]{1,0:T(1,128)} %broadcast_in_dim.21.ids_ref), custom_call_target="tpu_custom_call" | custom-call | tf_op jit(solution)/shard_map/pallas_call | solution.py:142
  8.1 81.8 %shard_map.87 = (bf16[1024,3072]{1,0:T(8,128)(2,1)}, bf16[1024,1024]{1,0:T(8,128)(2,1)}, bf16[7,384,1024]{2,1,0:T(8,128)(2,1)}, bf16[192,8,512]{2,1,0:T(8,128)(2...) custom-call(bf16[384,1024]{1,0:T(8,128)(2,1)} %tok_ref.3, bf16[16,768]{1,0:T(8,128)(2,1)} %win_ref.1, ...), custom_call_target="tpu_custom_call" | custom-call | tf_op jit(solution)/shard_map/pallas_call | solution.py:549
  90.0 79.0 %shard_map.88 = (bf16[384,1024]{1,0:T(8,128)(2,1)}, bf16[192,8192]{1,0:T(8,128)(2,1)}) custom-call(s32[8]{0:T(128)} %pad_add_fusion.bounds, bf16[2688,1024]{1,0:T(8,128)(2,1)} %bitcast.8, bf16[1024,3072]{1,0:T(8,128)(2,1)} %get-tuple-element.12.wqkv_hbm, bf16[1024,1024]{1,0:T(8,128)(2,1)} %get-tuple-element.13.wo_hbm, s32[1,3968]{1,0:T(1,128)} %broadcast_in_dim.21.ids_ref, ...), custom_call_target="tpu_custom_call" | custom-call | tf_op jit(solution)/shard_map/pallas_call | solution.py:287
  (5 shorter events, 0.0 us)

commit v3 on v2

--- a/solution.py
+++ b/solution.py
@@ -106,12 +106,15 @@
     return high, place - 32.0 * high
 
 
-def slots_kernel(tok_ref, owner_row, owner_col, ids_ref, slots_ref, info_ref, wide, stage, place_all):
+def slots_kernel(tok_ref, owner_row, ids_ref, slots_ref, info_ref, wide, stage, place_all):
     pages = BLK // PAGE
-    same = owner_col[...] == owner_row[...]
+    owner = owner_row[...].astype(F32)
+    eye = iota((pages, pages), 0) == iota((pages, pages), 1)
+    owner_col = jnp.sum(jnp.where(eye, jnp.broadcast_to(owner, (pages, pages)), 0.0), axis=1, keepdims=True)
+    same = owner_col == owner
     earlier = iota((pages, pages), 0) < iota((pages, pages), 1)
     rank = jnp.sum(jnp.where(same & earlier, 1.0, 0.0), axis=0, keepdims=True)
-    target = owner_row[...].astype(F32) * CAP + rank
+    target = owner * CAP + rank
     hot = jnp.where(iota((N_TOK * CAP, pages), 0).astype(F32) == target, 1.0, 0.0).astype(BF)
     for k in range(D // 128):
         wide[k] = tok_ref[:, k * 128 : k * 128 + 128].astype(F32)
@@ -138,21 +141,21 @@
     info_ref[...] = info[:, None, :]
 
 
-def build_slots(tokens, owner_row, owner_col, ids_row):
+def build_slots(tokens, owner_row, ids_row):
     return pl.pallas_call(
         slots_kernel,
         out_shape=(
             jax.ShapeDtypeStruct((N_TOK * CAP * 8, 512), BF),
             jax.ShapeDtypeStruct((N_TOK, 1, 128), F32),
         ),
-        in_specs=[VMEM] * 4,
+        in_specs=[VMEM] * 3,
         out_specs=[VMEM] * 2,
         scratch_shapes=[
             pltpu.VMEM((D // 128, BLK, 128), F32),
             pltpu.VMEM((4, N_TOK * CAP * 8, 128), F32),
             pltpu.VMEM((BLK, 128), F32),
         ],
-    )(tokens, owner_row, owner_col, ids_row)
+    )(tokens, owner_row, ids_row)
 
 
 PAIRS = 2
@@ -160,10 +163,15 @@
 
 def main_kernel(bounds, window_ref, wqkv_hbm, wo_hbm, ids_ref, gain_ref, tab_ref, slots_hbm, info_ref,
                 out_ref, cache_ref,
-                tok, wqkv, wo, keys, values, heads, scores, mixed, slots, stage, sems):
+                tok, wqkv, wo, keys, values, marks, heads, scores, mixed, slots, stage, sems):
+    own = pl.ds(REACH * BLK, BLK)
+    before, after = pl.ds(0, REACH * BLK), pl.ds((REACH + 1) * BLK, REACH * BLK)
     copies = [
-        pltpu.make_async_copy(window_ref, tok.at[pl.ds(0, WIN)], sems.at[0]),
-        pltpu.make_async_copy(wqkv_hbm, wqkv, sems.at[1]),
+        pltpu.make_async_copy(window_ref.at[own], tok.at[own], sems.at[0]),
+        pltpu.make_async_copy(wqkv_hbm.at[:, :D], wqkv.at[:, :D], sems.at[1]),
+        pltpu.make_async_copy(wqkv_hbm.at[:, D:], wqkv.at[:, D:], sems.at[4]),
+        pltpu.make_async_copy(window_ref.at[before], tok.at[before], sems.at[5]),
+        pltpu.make_async_copy(window_ref.at[after], tok.at[after], sems.at[6]),
         pltpu.make_async_copy(slots_hbm, slots, sems.at[2]),
         pltpu.make_async_copy(wo_hbm, wo, sems.at[3]),
     ]
@@ -180,11 +188,13 @@
         cosine, sine = turn(*split_place(place), tab_ref)
         part = mm(normed, wqkv[:, :D])
         for pair in range(H // 2):
-            turned = rotated(part[:, pair * 128 : pair * 128 + 128], cosine, sine).astype(BF) * BF(0.125)
-            left = iota((128, 128), 1) < 64
-            none = jnp.zeros((128, 128), BF)
-            heads[t, pair, :128, :] = jnp.where(left, turned, none)
-            heads[t, pair, 128:, :] = jnp.where(left, none, turned)
+            turned = rotated(part[:, pair * 128 : pair * 128 + 128], cosine, sine)
+            turned = turned.T.astype(BF).astype(F32) * 0.125
+            upper = iota((128, 128), 0) < 64
+            heads[t, pair, :, :128] = jnp.where(upper, turned, 0.0).astype(BF)
+            heads[t, pair, :, 128:] = jnp.where(upper, 0.0, turned).astype(BF)
+    for k in range(2, 5):
+        copies[k].wait()
     low = bounds[0]
     count = (bounds[5] + 2 - low) // 2
 
@@ -195,20 +205,27 @@
         local = start + iota((256, 1), 0)
         real = (local < WIN) & (local + first_row >= REACH * BLK) & (local + first_row < N_TOK * 4 * BLK + REACH * BLK)
         normed = jnp.where(real, layer_norm(tok[here, :].astype(F32), gain), 0.0).astype(BF)
-        place = jnp.concatenate([ids_and_places(ids_ref, chunk)[1], ids_and_places(ids_ref, chunk + 1)[1]], axis=0)
+        pieces = [ids_and_places(ids_ref, chunk + k) for k in range(2)]
+        place = jnp.concatenate([p[1] for p in pieces], axis=0)
+        for k in range(2):
+            marks[pl.ds(pl.multiple_of(start + k * 128, 128), 128), :] = jnp.broadcast_to(pieces[k][0], (128, 128))
         cosine, sine = turn(*split_place(place), tab_ref)
         for part in range(2):
             got = mm(normed, wqkv[:, D + part * 512 : D + part * 512 + 512])
             for k in range(4):
                 lanes = pl.ds(part * 512 + k * 128, 128)
                 keys[here, lanes] = rotated(got[:, k * 128 : k * 128 + 128], cosine, sine).astype(BF)
-        values[here, :] = mm(normed, wqkv[:, 2 * D :]).astype(BF)
+        for part in range(2):
+            got = mm(normed, wqkv[:, 2 * D + part * 512 : 2 * D + part * 512 + 512])
+            for k in range(4):
+                lane = part * 512 + k * 128
+                values[pl.ds(lane, 128), here] = got[:, k * 128 : k * 128 + 128].T.astype(BF)
         return 0
 
     lax.fori_loop(0, count, project, 0)
+    fold = lambda op, value: op(value.reshape(32, 8, 128), axis=0)
     for t in range(3):
-        id_col = column(ids_ref[:, pl.ds(SPAN + REACH * BLK + t * 128, 128)].astype(F32))
-        id_col = jnp.concatenate([id_col, id_col], axis=0)
+        id_row = ids_ref[:, pl.ds(SPAN + REACH * BLK + t * 128, 128)].astype(F32)
         begin = bounds[t]
         steps = (bounds[3 + t] - begin + 1) // 2
 
@@ -217,45 +234,46 @@
 
             def score(i, peaks):
                 start = pl.multiple_of((begin + i * 2) * 128, 128)
-                id_row = ids_ref[:, pl.ds(pl.multiple_of(start + SPAN, 128), 256)].astype(F32)
-                allowed = id_col == id_row
+                allowed = marks[pl.ds(start, 256), :] == id_row
                 new = []
                 for j in range(PAIRS):
-                    got = lax.dot_general(
-                        heads[t, group * PAIRS + j], keys[pl.ds(start, 256), pl.ds(lane0[j], 128)],
-                        (((1,), (1,)), ((), ())), preferred_element_type=F32)
-                    got = jnp.where(allowed, got, NEG_FILL)
-                    scores[j, i] = got
-                    new.append(jnp.maximum(peaks[j], jnp.maximum(got[:, :128], got[:, 128:])))
+                    got = mm(keys[pl.ds(start, 256), pl.ds(lane0[j], 128)], heads[t, group * PAIRS + j])
+                    for side in range(2):
+                        half = jnp.where(allowed, got[:, side * 128 : side * 128 + 128], NEG_FILL)
+                        scores[j, i, side] = half
+                        new.append(jnp.maximum(peaks[2 * j + side], fold(jnp.max, half)))
                 return tuple(new)
 
-            peaks = lax.fori_loop(0, steps, score, (jnp.full((256, 128), NEG_FILL, F32),) * PAIRS)
-            peaks = [jnp.max(p, axis=1, keepdims=True) for p in peaks]
+            peaks = lax.fori_loop(0, steps, score, (jnp.full((8, 128), NEG_FILL, F32),) * (2 * PAIRS))
+            peaks = [jnp.max(p, axis=0, keepdims=True) for p in peaks]
 
             def mix(i, carry):
                 start = pl.multiple_of((begin + i * 2) * 128, 128)
-                new = []
+                totals, accs = [], []
                 for j in range(PAIRS):
-                    total, acc = carry[j]
-                    weight = jnp.exp(scores[j, i] - peaks[j])
-                    total = total + weight[:, :128] + weight[:, 128:]
-                    acc = acc + mm(weight.astype(BF), values[pl.ds(start, 256), pl.ds(lane0[j], 128)])
-                    new.append((total, acc))
-                return tuple(new)
-
-            zero = jnp.zeros((256, 128), F32)
-            done = lax.fori_loop(0, steps, mix, ((zero, zero),) * PAIRS)
+                    both = []
+                    for side in range(2):
+                        weight = jnp.exp(scores[j, i, side] - peaks[2 * j + side])
+                        totals.append(carry[2 * j + side] + fold(jnp.sum, weight))
+                        both.append(weight.astype(BF))
+                    accs.append(carry[2 * PAIRS + j] + mm(
+                        values[pl.ds(lane0[j], 128), pl.ds(start, 256)], jnp.concatenate(both, axis=1)))
+                return tuple(totals + accs)
+
+            done = lax.fori_loop(
+                0, steps, mix, (jnp.zeros((8, 128), F32),) * (2 * PAIRS) + (jnp.zeros((128, 256), F32),) * PAIRS)
             for j in range(PAIRS):
-                total, acc = done[j]
-                acc = acc / jnp.sum(total, axis=1, keepdims=True)
-                left = iota((128, 128), 1) < 64
-                mixed[pl.ds(t * 128, 128), pl.ds(lane0[j], 128)] = jnp.where(left, acc[:128], acc[128:]).astype(BF)
+                total = [jnp.sum(done[2 * j + side], axis=0, keepdims=True) for side in range(2)]
+                acc = done[2 * PAIRS + j]
+                upper = iota((128, 128), 0) < 64
+                picked = jnp.where(upper, acc[:, :128] / total[0], acc[:, 128:] / total[1])
+                mixed[pl.ds(t * 128, 128), pl.ds(lane0[j], 128)] = picked.T.astype(BF)
             return 0
 
         lax.fori_loop(0, H // 2 // PAIRS, pairs, 0)
-    copies[3].wait()
+    copies[6].wait()
     out_ref[...] = mm(mixed[...], wo[...]).astype(BF)
-    copies[2].wait()
+    copies[5].wait()
     for k in range(4):
         stage[k] = slots[:, k * 128 : k * 128 + 128].astype(F32)
     count_slots = N_TOK * CAP
@@ -297,13 +315,14 @@
             pltpu.VMEM((D, 3 * D), BF),
             pltpu.VMEM((D, D), BF),
             pltpu.VMEM((WIN + EXTRA, D), BF),
-            pltpu.VMEM((WIN + EXTRA, D), BF),
-            pltpu.VMEM((3, H // 2, 256, 128), BF),
-            pltpu.VMEM((PAIRS, 11, 256, 256), F32),
+            pltpu.VMEM((D, WIN + EXTRA), BF),
+            pltpu.VMEM((WIN + EXTRA, 128), F32),
+            pltpu.VMEM((3, H // 2, 128, 256), BF),
+            pltpu.VMEM((PAIRS, 11, 2, 256, 128), F32),
             pltpu.VMEM((BLK, D), BF),
             pltpu.VMEM((N_TOK * CAP * 8, 512), BF),
             pltpu.VMEM((4, N_TOK * CAP * 8, 128), F32),
-            pltpu.SemaphoreType.DMA((4,)),
+            pltpu.SemaphoreType.DMA((7,)),
         ],
         compiler_params=pltpu.CompilerParams(vmem_limit_bytes=60 * 1024 * 1024),
     )(bounds, window, wqkv, wo, ids_row, gain, tables, slots, info)
@@ -312,6 +331,9 @@
 def remote(src, dst, ssem, rsem, tok, grp):
     return pltpu.make_async_remote_copy(src_ref=src, dst_ref=dst, send_sem=ssem, recv_sem=rsem,
                                         device_id=(tok, grp), device_id_type=MESH)
+
+CUT = (1, 12, 20, 28, 36, 64)
+
 
 def comm_kernel(tok_ref, win_ref, wout_ref, slots_ref, place_ref,
                 wqkv_ref, wo_ref, window_ref, slots_out, place_out, outer_ref,
@@ -455,20 +477,20 @@
     if do["pages"]:
         pltpu.make_async_copy(slots_ref.at[mine], slots_out.at[mine], loc.at[3]).start()
         pltpu.make_async_copy(place_ref.at[a], place_out.at[a], loc.at[4]).start()
-    send_pages(1, 12)
+    send_pages(CUT[0], CUT[1])
     if do["weights"]:
         for w in W: pltpu.make_async_copy(shard[w], piece(w, a, x), loc.at[w]).wait()
         z_step(1); joins(0)
-    send_pages(12, 20)
+    send_pages(CUT[1], CUT[2])
     if do["weights"]:
         z_step(2); joins(1)
-    send_pages(20, 28)
+    send_pages(CUT[2], CUT[3])
     if do["weights"]: z_step(3)
     if do["tokens"]: outer_on()
-    send_pages(28, 36)
+    send_pages(CUT[3], CUT[4])
     if do["weights"]:
         joins(2); z_step(4)
-    send_pages(36, 64)
+    send_pages(CUT[4], CUT[5])
     if do["tokens"]: ring_relay()
     if do["weights"]:
         joins(3)
@@ -573,7 +595,7 @@
     end = (jnp.sum((reach[None, :] <= own[:, 127:]).astype(jnp.int32), axis=1) + 127) // 128
     bounds = jnp.concatenate([begin, end, first_row[None], first_row[None]])
     ids_row = ids[None, :]
-    slots, info = build_slots(tokens, page_owner.reshape(1, -1), page_owner, ids_row)
+    slots, info = build_slots(tokens, page_owner.reshape(1, -1), ids_row)
     wqkv, wo, window, slots, info = comm(tokens, input_weight, output_weight, slots.reshape(N_TOK * CAP, 8, 512), info)
     return main_call(bounds, window.reshape(WIN, D), wqkv, wo, ids_row, norm_gain[None, :], tables,
                      slots.reshape(N_TOK * CAP * 8, 512), info)

time: 169 us -> 158 us (0.935)
  the two profiles are of different devices: /device:TPU:14 before, /device:TPU:8 now
where the time goes in v3:
time: 158 us
  Pallas kernels  154 us (97%)
  other arithmetic  1.64 us (1%)
    pallas_call x1, Pallas kernels, comm(): pl.pallas_call(comm_kernel, out_shape=(jax.ShapeDtypeStruct((1024, 3072),...  83.3 us
    pallas_call x1, Pallas kernels, main_call(): pl.pallas_call(main_kernel, out_shape=(jax.ShapeDtypeStruct((BLK, D), BF)...  67.6 us
    pallas_call x1, Pallas kernels, build_slots(): pl.pallas_call(slots_kernel, out_shape=(jax.ShapeDtypeStruct((N_TOK * CAP...  3.53 us

profile of v3, /device:TPU:8, one launch (start us, length us, event | category | flops | bytes accessed | tf_op | source)
XLA Modules:
  0.0 157.7 jit_solution(415371984624030715)
XLA Ops:
  0.7 0.8 fusion.1
  1.5 0.2 slice_reduce_fusion.1
  1.7 0.2 convert_reduce_fusion.1
  1.9 0.6 broadcast_in_dim.21.ids_ref
  2.6 0.6 pad_add_fusion.bounds
  3.1 3.5 %shard_map.86 = (bf16[1536,512]{1,0:T(8,128)(2,1)}, f32[64,1,128]{2,1,0:T(1,128)}) custom-call(bf16[384,1024]{1,0:T(8,128)(2,1)} %tok_ref.3, s32[1,96]{1,0:T(1,128)} %bitcast.12, s32[1,3968]{1,0:T(1,128)} %broadcast_in_dim.21.ids_ref), custom_call_target="tpu_custom_call" | custom-call | tf_op jit(solution)/shard_map/pallas_call | solution.py:145
  6.7 83.3 %shard_map.87 = (bf16[1024,3072]{1,0:T(8,128)(2,1)}, bf16[1024,1024]{1,0:T(8,128)(2,1)}, bf16[7,384,1024]{2,1,0:T(8,128)(2,1)}, bf16[192,8,512]{2,1,0:T(8,128)(2...) custom-call(bf16[384,1024]{1,0:T(8,128)(2,1)} %tok_ref.3, bf16[16,768]{1,0:T(8,128)(2,1)} %win_ref.1, ...), custom_call_target="tpu_custom_call" | custom-call | tf_op jit(solution)/shard_map/pallas_call | solution.py:571
  90.0 67.6 %shard_map.88 = (bf16[384,1024]{1,0:T(8,128)(2,1)}, bf16[192,8192]{1,0:T(8,128)(2,1)}) custom-call(s32[8]{0:T(128)} %pad_add_fusion.bounds, bf16[2688,1024]{1,0:T(8,128)(2,1)} %bitcast.8, bf16[1024,3072]{1,0:T(8,128)(2,1)} %get-tuple-element.12.wqkv_hbm, bf16[1024,1024]{1,0:T(8,128)(2,1)} %get-tuple-element.13.wo_hbm, s32[1,3968]{1,0:T(1,128)} %broadcast_in_dim.21.ids_ref, ...), custom_call_target="tpu_custom_call" | custom-call | tf_op jit(solution)/shard_map/pallas_call | solution.py:305
  (5 shorter events, 0.0 us)

commit v4 on v3

--- a/solution.py
+++ b/solution.py
@@ -158,7 +158,7 @@
     )(tokens, owner_row, ids_row)
 
 
-PAIRS = 2
+PAIRS = 4
 
 
 def main_kernel(bounds, window_ref, wqkv_hbm, wo_hbm, ids_ref, gain_ref, tab_ref, slots_hbm, info_ref,

time: 158 us -> 147 us (0.930)
  the two profiles are of different devices: /device:TPU:8 before, /device:TPU:65 now
where the time goes in v4:
time: 147 us; the launch traced here: 146 us
  Pallas kernels  143 us (97%)
  other arithmetic  1.64 us (1%)
    pallas_call x1, Pallas kernels, comm(): pl.pallas_call(comm_kernel, out_shape=(jax.ShapeDtypeStruct((1024, 3072),...  83 us
    pallas_call x1, Pallas kernels, main_call(): pl.pallas_call(main_kernel, out_shape=(jax.ShapeDtypeStruct((BLK, D), BF)...  56.7 us
    pallas_call x1, Pallas kernels, build_slots(): pl.pallas_call(slots_kernel, out_shape=(jax.ShapeDtypeStruct((N_TOK * CAP...  3.53 us

profile of v4, /device:TPU:65, one launch (start us, length us, event | category | flops | bytes accessed | tf_op | source)
XLA Modules:
  0.0 146.5 jit_solution(5746645568476745713)
XLA Ops:
  0.7 0.8 fusion.1
  1.5 0.2 slice_reduce_fusion.1
  1.7 0.2 convert_reduce_fusion.1
  1.9 0.6 broadcast_in_dim.21.ids_ref
  2.6 0.6 pad_add_fusion.bounds
  3.1 3.5 %shard_map.86 = (bf16[1536,512]{1,0:T(8,128)(2,1)}, f32[64,1,128]{2,1,0:T(1,128)}) custom-call(bf16[384,1024]{1,0:T(8,128)(2,1)} %tok_ref.3, s32[1,96]{1,0:T(1,128)} %bitcast.12, s32[1,3968]{1,0:T(1,128)} %broadcast_in_dim.21.ids_ref), custom_call_target="tpu_custom_call" | custom-call | tf_op jit(solution)/shard_map/pallas_call | solution.py:145
  6.7 83.0 %shard_map.87 = (bf16[1024,3072]{1,0:T(8,128)(2,1)}, bf16[1024,1024]{1,0:T(8,128)(2,1)}, bf16[7,384,1024]{2,1,0:T(8,128)(2,1)}, bf16[192,8,512]{2,1,0:T(8,128)(2...) custom-call(bf16[384,1024]{1,0:T(8,128)(2,1)} %tok_ref.3, bf16[16,768]{1,0:T(8,128)(2,1)} %win_ref.1, ...), custom_call_target="tpu_custom_call" | custom-call | tf_op jit(solution)/shard_map/pallas_call | solution.py:571
  89.7 56.7 %shard_map.88 = (bf16[384,1024]{1,0:T(8,128)(2,1)}, bf16[192,8192]{1,0:T(8,128)(2,1)}) custom-call(s32[8]{0:T(128)} %pad_add_fusion.bounds, bf16[2688,1024]{1,0:T(8,128)(2,1)} %bitcast.8, bf16[1024,3072]{1,0:T(8,128)(2,1)} %get-tuple-element.12.wqkv_hbm, bf16[1024,1024]{1,0:T(8,128)(2,1)} %get-tuple-element.13.wo_hbm, s32[1,3968]{1,0:T(1,128)} %broadcast_in_dim.21.ids_ref, ...), custom_call_target="tpu_custom_call" | custom-call | tf_op jit(solution)/shard_map/pallas_call | solution.py:305
  (5 shorter events, 0.0 us)

commit v5 on v4

--- a/solution.py
+++ b/solution.py
@@ -158,7 +158,7 @@
     )(tokens, owner_row, ids_row)
 
 
-PAIRS = 4
+PAIRS = 8
 
 
 def main_kernel(bounds, window_ref, wqkv_hbm, wo_hbm, ids_ref, gain_ref, tab_ref, slots_hbm, info_ref,
@@ -318,13 +318,13 @@
             pltpu.VMEM((D, WIN + EXTRA), BF),
             pltpu.VMEM((WIN + EXTRA, 128), F32),
             pltpu.VMEM((3, H // 2, 128, 256), BF),
-            pltpu.VMEM((PAIRS, 11, 2, 256, 128), F32),
+            pltpu.VMEM((PAIRS, 9, 2, 256, 128), F32),
             pltpu.VMEM((BLK, D), BF),
             pltpu.VMEM((N_TOK * CAP * 8, 512), BF),
             pltpu.VMEM((4, N_TOK * CAP * 8, 128), F32),
             pltpu.SemaphoreType.DMA((7,)),
         ],
-        compiler_params=pltpu.CompilerParams(vmem_limit_bytes=60 * 1024 * 1024),
+        compiler_params=pltpu.CompilerParams(vmem_limit_bytes=67043328),
     )(bounds, window, wqkv, wo, ids_row, gain, tables, slots, info)
 
 

time: 147 us -> 141 us (0.959)
  the two profiles are of different devices: /device:TPU:65 before, /device:TPU:1 now
where the time goes in v5:
time: 141 us
  Pallas kernels  138 us (98%)
  other arithmetic  1.63 us (1%)
    pallas_call x1, Pallas kernels, comm(): pl.pallas_call(comm_kernel, out_shape=(jax.ShapeDtypeStruct((1024, 3072),...  85.4 us
    pallas_call x1, Pallas kernels, main_call(): pl.pallas_call(main_kernel, out_shape=(jax.ShapeDtypeStruct((BLK, D), BF)...  49.1 us
    pallas_call x1, Pallas kernels, build_slots(): pl.pallas_call(slots_kernel, out_shape=(jax.ShapeDtypeStruct((N_TOK * CAP...  3.53 us

profile of v5, /device:TPU:1, one launch (start us, length us, event | category | flops | bytes accessed | tf_op | source)
XLA Modules:
  0.0 141.3 jit_solution(3636539125203770615)
XLA Ops:
  0.7 0.8 fusion.1
  1.5 0.2 slice_reduce_fusion.1
  1.7 0.2 convert_reduce_fusion.1
  1.9 0.6 broadcast_in_dim.21.ids_ref
  2.6 0.6 pad_add_fusion.bounds
  3.1 3.5 %shard_map.86 = (bf16[1536,512]{1,0:T(8,128)(2,1)}, f32[64,1,128]{2,1,0:T(1,128)}) custom-call(bf16[384,1024]{1,0:T(8,128)(2,1)} %tok_ref.3, s32[1,96]{1,0:T(1,128)} %bitcast.12, s32[1,3968]{1,0:T(1,128)} %broadcast_in_dim.21.ids_ref), custom_call_target="tpu_custom_call" | custom-call | tf_op jit(solution)/shard_map/pallas_call | solution.py:145
  6.7 85.4 %shard_map.87 = (bf16[1024,3072]{1,0:T(8,128)(2,1)}, bf16[1024,1024]{1,0:T(8,128)(2,1)}, bf16[7,384,1024]{2,1,0:T(8,128)(2,1)}, bf16[192,8,512]{2,1,0:T(8,128)(2...) custom-call(bf16[384,1024]{1,0:T(8,128)(2,1)} %tok_ref.3, bf16[16,768]{1,0:T(8,128)(2,1)} %win_ref.1, ...), custom_call_target="tpu_custom_call" | custom-call | tf_op jit(solution)/shard_map/pallas_call | solution.py:571
  92.0 49.1 %shard_map.88 = (bf16[384,1024]{1,0:T(8,128)(2,1)}, bf16[192,8192]{1,0:T(8,128)(2,1)}) custom-call(s32[8]{0:T(128)} %pad_add_fusion.bounds, bf16[2688,1024]{1,0:T(8,128)(2,1)} %bitcast.8, bf16[1024,3072]{1,0:T(8,128)(2,1)} %get-tuple-element.12.wqkv_hbm, bf16[1024,1024]{1,0:T(8,128)(2,1)} %get-tuple-element.13.wo_hbm, s32[1,3968]{1,0:T(1,128)} %broadcast_in_dim.21.ids_ref, ...), custom_call_target="tpu_custom_call" | custom-call | tf_op jit(solution)/shard_map/pallas_call | solution.py:305
  (5 shorter events, 0.0 us)
